TPU v7x, 32 devices: a whole 2x2x4 slice. The times are simulated.
32 devices in a mesh: frow: 4 (over x, core), fcol: 8 (over z, y).
Axes of the slice: x: 2, y: 2, z: 4, core: 2. Of those that a mesh axis runs over, the one named last changes fastest.
Arguments:
- facet_image: bfloat16 [2048, 4096], P('frow', 'fcol'), may hold values from -6 to 6
- row_offsets: int32 [2], replicated, may hold values from 0 to 65280
- col_offsets: int32 [2], replicated, may hold values from 0 to 65280
- vis_subgrid: int32 [16384], P(('frow', 'fcol')), may hold values from 0 to 3
- vis_u: int32 [16384], P(('frow', 'fcol')), may hold values from 0 to 255
- vis_v: int32 [16384], P(('frow', 'fcol')), may hold values from 0 to 255
- observed: float32 [2, 16384], P(None, ('frow', 'fcol')), may hold values from -6 to 6
Outputs:
- facet_residual: float32 [2048, 4096], P('frow', 'fcol')
- residual_vis: float32 [2, 16384], P(None, ('frow', 'fcol'))
Inputs may be any that keep to these rules, and one draw needn't show every extreme that they name: `vis_subgrid`: subgrid numbers count row by row over the 2 x 2 subgrids.
All inputs are finite; a program needn't handle non-finite values.
Results may differ from a plain program's by a relative error of at most 0.023.
Values may be sent and summed in bfloat16 or wider, within the bound.
A program may use at most 64 MiB of HBM per device.

v0:
```python
import functools
import math

import jax
import jax.numpy as jnp
from jax import lax
from jax.experimental import pallas as pl
from jax.experimental.pallas import tpu as pltpu
from jax.sharding import PartitionSpec as P

SKY = 65536
SG = 256
NR = 2
NC = 2
f32 = jnp.float32
bf16 = jnp.bfloat16
i32 = jnp.int32
MESH = pl.DeviceIdType.MESH
VM = pl.BlockSpec(memory_space=pltpu.VMEM)
SM = pl.BlockSpec(memory_space=pltpu.SMEM)
LIMIT = 60 << 20


def geometry():
    rows = lax.axis_size("frow")
    cols = lax.axis_size("fcol")
    nx = rows // 2
    ny = 1 << ((cols.bit_length() - 1) // 2)
    nz = cols // ny
    return rows, cols, nx, ny, nz


def position():
    _, _, _, ny, _ = geometry()
    frow = lax.axis_index("frow")
    fcol = lax.axis_index("fcol")
    return frow // 2, frow % 2, fcol % ny, fcol // ny


def dims(contract):
    return ((contract, contract), ((), ()))


def phase(product):
    angle = (product & (SKY - 1)).astype(f32) * (2.0 * math.pi / SKY)
    return jnp.cos(angle), jnp.sin(angle)


def expand(first, places, c_ref, s_ref):
    n = places.shape[1]
    steps = lax.broadcasted_iota(i32, (16, n), 0)
    c0, s0 = phase(steps * places)
    c1, s1 = phase((first + 16 * steps) * places)
    for k in range(SG // 16):
        ck = c1[k : k + 1]
        sk = s1[k : k + 1]
        c_ref[k * 16 : k * 16 + 16, :] = (ck * c0 - sk * s0).astype(bf16)
        s_ref[k * 16 : k * 16 + 16, :] = (sk * c0 + ck * s0).astype(bf16)


def place(q):
    _, _, _, ny, nz = geometry()
    return q // (ny * nz), (q // nz) % ny, q % nz


def device(q, h):
    _, _, _, ny, _ = geometry()
    x, y, z = place(q)
    return (2 * x + h, z * ny + y)


def hots(vis, h, base, rows_own):
    n = vis.shape[1]
    cell = vis[0:1].astype(i32)
    sub = cell // (SG * SG)
    row = (sub // NC) * SG + (cell // SG) % SG - base
    row = jnp.where(sub % NC == h, row, -1)
    hot_row = lax.broadcasted_iota(i32, (rows_own, n), 0) == row
    hot_col = lax.broadcasted_iota(i32, (SG, n), 0) == cell % SG
    return hot_row, jnp.where(hot_col, 1.0, 0.0).astype(bf16)


def main_kernel(
    scale, ro_ref, co_ref, sub_ref, u_ref, v_ref, obs_ref, facet_ref,
    g_ref, ar_ref, ai_ref, bt_ref, res_ref,
    kk, ks, rc, rs, vis_ref, vis_all, other, z_ref, zb_ref, grid_acc,
    acc_a, acc_b, send_a, send_b, got_a1, got_b1, got_a2, got_b2,
    own_z, send_z, got_z, gz, model, vals, pair_vals, slots,
    ssem, rsem, vs, vr, ws, wr, lsem,
):
    rows, cols, nx, ny, nz = geometry()
    x, h, y, z = position()
    chips = nx * ny * nz
    me = (x * ny + y) * nz + z
    fs = facet_ref.shape[0]
    nv = vis_ref.shape[1]
    rows_own = NR * SG // chips
    sib = (2 * x + 1 - h, lax.axis_index("fcol"))
    barrier = pltpu.get_barrier_semaphore()

    def peers(act):
        def step(d, carry):
            act(d, lax.rem(me + d, chips), lax.rem(me - d + chips, chips))
            return carry

        lax.fori_loop(1, chips, step, 0)

    peers(lambda d, to, frm: pl.semaphore_signal(barrier, inc=1, device_id=device(to, h), device_id_type=MESH))
    pl.semaphore_signal(barrier, inc=1, device_id=sib, device_id_type=MESH)
    cell = (sub_ref[...] * SG + u_ref[...]) * SG + v_ref[...]
    vis_ref[0:1] = cell.astype(f32)
    vis_ref[1:3] = obs_ref[...]
    vis_ref[3:4] = jnp.zeros((1, nv), f32)
    mine = pltpu.make_async_copy(vis_ref, vis_all.at[h, me], lsem)
    mine.start()
    expand(0, lax.broadcasted_iota(i32, (1, SG), 1) * (SKY // SG), kk, ks)
    used = [0]
    sent = []

    def send(src, dst, to):
        k = used[0]
        used[0] += 1
        copy = pltpu.make_async_remote_copy(
            src, dst, ssem.at[k], rsem.at[k], device_id=to, device_id_type=MESH
        )
        copy.start()
        sent.append(copy)
        return k

    def land(k, dst):
        pltpu.make_async_remote_copy(
            dst, dst, ssem.at[k], rsem.at[k], device_id=sib, device_id_type=MESH
        ).wait_recv()

    def link(d, to, slot):
        return pltpu.make_async_remote_copy(
            vis_ref, vis_all.at[h, slot], vs.at[d], vr.at[d],
            device_id=device(to, h), device_id_type=MESH,
        )


    kcos = kk[...]
    ksin = ks[...]
    wide = SG // 2
    waves = range(2)

    def compose(n, start, unit):
        places = (start + lax.broadcasted_iota(i32, (1, n), 1)) * unit
        expand(0, places, rc.at[:, :n], rs.at[:, :n])
        c = rc[:, :n]
        s = rs[:, :n]
        re = jnp.dot(kcos, c, preferred_element_type=f32) + jnp.dot(ksin, s, preferred_element_type=f32)
        im = jnp.dot(ksin, c, preferred_element_type=f32) - jnp.dot(kcos, s, preferred_element_type=f32)

        def shifted(offset):
            cos, sin = phase(offset * places)
            return (re * cos + im * sin).astype(bf16), (im * cos - re * sin).astype(bf16)

        return shifted

    shifted = compose(fs, lax.axis_index("fcol") * fs, SKY // (cols * fs))
    for c in range(NC):
        bt_ref[c, :SG], bt_ref[c, SG:] = shifted(co_ref[c])
    pl.semaphore_wait(barrier, chips)
    k_facet = send(facet_ref, other, sib)
    peers(lambda d, to, frm: link(d, to, me).start())
    shifted = compose(2 * fs, x * (2 * fs), SKY // (rows * fs))
    for r in range(NR):
        cut = slice(r * SG, r * SG + SG)
        ar_ref[cut], ai_ref[cut] = shifted(ro_ref[r])

    mine.wait()

    def project(ref, w):
        re = bt_ref[h, w * wide : (w + 1) * wide]
        im = bt_ref[h, SG + w * wide : SG + (w + 1) * wide]
        b = jnp.concatenate([re, im], 0)
        return lax.dot_general(ref[...], b, (((1,), (1,)), ((), ())), preferred_element_type=f32).astype(bf16)

    part = NR * SG // (nx * ny)
    own_cut = pl.ds(pl.multiple_of(h * fs, fs), fs)
    other_cut = pl.ds(pl.multiple_of((1 - h) * fs, fs), fs)
    first_a, first_b, second_a, second_b = [[], []], [[], []], [[], []], [[], []]
    third, fourth, fifth_a, fifth_b = [[], []], [[], []], [[], []], [[], []]
    sixth_a, sixth_b = [[], []], [[], []]

    def to_x(d):
        return device((lax.rem(x + d, nx) * ny + y) * nz + z, h)

    def to_y(d):
        return device((x * ny + lax.rem(y + d, ny)) * nz + z, h)

    def to_z(d):
        return device((x * ny + y) * nz + lax.rem(z + d, nz), h)

    for w in waves:
        own_p = project(facet_ref, w)
        if w == 0:
            land(k_facet, other)
        other_p = project(other, w)
        for dx in list(range(1, nx)) + [0]:
            px = lax.rem(x + dx, nx)
            for dy in list(range(1, ny)) + [0]:
                py = lax.rem(y + dy, ny)
                cut = pl.ds(pl.multiple_of((px * ny + py) * part, part), part)
                one = jnp.dot(ar_ref[cut, own_cut], own_p, preferred_element_type=f32)
                one += jnp.dot(ar_ref[cut, other_cut], other_p, preferred_element_type=f32)
                two = jnp.dot(ai_ref[cut, own_cut], own_p, preferred_element_type=f32)
                two += jnp.dot(ai_ref[cut, other_cut], other_p, preferred_element_type=f32)
                zr = one[:, :wide] - two[:, wide:]
                zi = one[:, wide:] + two[:, :wide]
                z_ref[w, 0, px, py] = zr
                z_ref[w, 1, px, py] = zi
                zb_ref[w, 0, px, py] = zr.astype(bf16)
                zb_ref[w, 1, px, py] = zi.astype(bf16)
                if dx == 0 and dy > 0:
                    first_b[w].append(send(zb_ref.at[w, 1, :, py], got_b1.at[w, dy - 1], to_y(dy)))
            if dx > 0:
                first_a[w].append(send(zb_ref.at[w, 0, px], got_a1.at[w, dx - 1], to_x(dx)))

    peers(lambda d, to, frm: link(d, to, frm).wait_recv())
    k_vis = send(vis_all.at[h], vis_all.at[h], sib)

    base = me * rows_own
    grid_acc[...] = jnp.zeros_like(grid_acc)

    def gridding(side, lo, hi):
        def one(q):
            vis = vis_all[side, q]
            hot_row, hot_col = hots(vis, h, base, rows_own)
            parts = []
            for p in (1, 2):
                val = vis[p : p + 1]
                high = val.astype(bf16).astype(f32)
                parts += [high, val - high]
            parts.append(jnp.ones_like(vis[0:1]))
            left = jnp.concatenate([jnp.where(hot_row, t, 0.0) for t in parts], 0).astype(bf16)
            return lax.dot_general(left, hot_col, (((1,), (1,)), ((), ())), preferred_element_type=f32)

        def body(t, carry):
            got = one(lo + 2 * t) + one(lo + 2 * t + 1)
            grid_acc[...] += got
            return carry

        lax.fori_loop(0, (hi - lo) // 2, body, 0)

    half = chips // 2

    def stage_two(w):
        for d in range(nx - 1):
            land(first_a[w][d], got_a1.at[w, d])
        total = z_ref[w, 0, x]
        for d in range(nx - 1):
            total = total + got_a1[w, d].astype(f32)
        acc_a[w] = total
        send_a[w] = total.astype(bf16)
        for d in range(1, ny):
            second_a[w].append(send(send_a.at[w, lax.rem(y + d, ny)], got_a2.at[w, d - 1], to_y(d)))
        for d in range(ny - 1):
            land(first_b[w][d], got_b1.at[w, d])
        total = z_ref[w, 1, :, y]
        for d in range(ny - 1):
            total = total + got_b1[w, d].astype(f32)
        acc_b[w] = total
        send_b[w] = total.astype(bf16)
        for d in range(1, nx):
            second_b[w].append(send(send_b.at[w, lax.rem(x + d, nx)], got_b2.at[w, d - 1], to_x(d)))

    def stage_three(w):
        for d in range(ny - 1):
            land(second_a[w][d], got_a2.at[w, d])
        re = acc_a[w, y]
        for d in range(ny - 1):
            re = re + got_a2[w, d].astype(f32)
        for d in range(nx - 1):
            land(second_b[w][d], got_b2.at[w, d])
        im = acc_b[w, x]
        for d in range(nx - 1):
            im = im + got_b2[w, d].astype(f32)
        for k in range(nz):
            cut = slice(k * rows_own, (k + 1) * rows_own)
            own_z[w, k, :, :wide] = re[cut]
            own_z[w, k, :, wide:] = im[cut]
            send_z[w, k, :, :wide] = re[cut].astype(bf16)
            send_z[w, k, :, wide:] = im[cut].astype(bf16)
        for d in range(1, nz):
            third[w].append(send(send_z.at[w, lax.rem(z + d, nz)], got_z.at[w, d - 1], to_z(d)))

    def turn(w):
        for d in range(nz - 1):
            land(third[w][d], got_z.at[w, d])
        total = own_z[w, z]
        for d in range(nz - 1):
            total = total + got_z[w, d].astype(f32)
        m = total * scale
        cut = slice(w * wide, (w + 1) * wide)
        got = [grid_acc[p * rows_own : (p + 1) * rows_own, cut] for p in range(5)]
        hat_re = got[0] + got[1] - got[4] * m[:, :wide]
        hat_im = got[2] + got[3] - got[4] * m[:, wide:]
        gz[w, z, :, :wide] = hat_re.astype(bf16)
        gz[w, z, :, wide:] = hat_im.astype(bf16)
        for d in range(1, nz):
            fourth[w].append(send(gz.at[w, z], gz.at[w, z], to_z(d)))
        both = jnp.concatenate([m[:, :wide], m[:, wide:]], 0)
        high = both.astype(bf16)
        model[: 2 * rows_own, cut] = high
        model[2 * rows_own :, cut] = (both - high.astype(f32)).astype(bf16)

    cross = []

    def over(index):
        src = g_ref.at[(h,) + index]
        cross.append((send(src, src, sib), index))

    def stage_five(w):
        for d in range(1, nz):
            land(fourth[w][d - 1], gz.at[w, lax.rem(z - d + nz, nz)])
        for k in range(nz):
            cut = slice(k * rows_own, (k + 1) * rows_own)
            g_ref[h, w, 0, x, y, cut, :] = gz[w, k, :, :wide]
            g_ref[h, w, 1, x, y, cut, :] = gz[w, k, :, wide:]
        for d in range(1, ny):
            blk = g_ref.at[h, w, 0, x, y]
            fifth_a[w].append(send(blk, blk, to_y(d)))
        for d in range(1, nx):
            blk = g_ref.at[h, w, 1, x, y]
            fifth_b[w].append(send(blk, blk, to_x(d)))
        over((w, 0, x, y))
        over((w, 1, x, y))

    def stage_six(w):
        for d in range(1, ny):
            land(fifth_a[w][d - 1], g_ref.at[h, w, 0, x, lax.rem(y - d + ny, ny)])
        for d in range(1, nx):
            blk = g_ref.at[h, w, 0, x]
            sixth_a[w].append(send(blk, blk, to_x(d)))
        for d in range(1, nx):
            land(fifth_b[w][d - 1], g_ref.at[h, w, 1, lax.rem(x - d + nx, nx), y])
        for d in range(1, ny):
            blk = g_ref.at[h, w, 1, :, y]
            sixth_b[w].append(send(blk, blk, to_y(d)))
        for d in range(1, ny):
            over((w, 0, x, lax.rem(y - d + ny, ny)))
        for d in range(1, nx):
            over((w, 1, lax.rem(x - d + nx, nx), y))

    def finish(w):
        for d in range(1, nx):
            px = lax.rem(x - d + nx, nx)
            land(sixth_a[w][d - 1], g_ref.at[h, w, 0, px])
            over((w, 0, px))
        for d in range(1, ny):
            py = lax.rem(y - d + ny, ny)
            land(sixth_b[w][d - 1], g_ref.at[h, w, 1, :, py])
            over((w, 1, slice(None), py))

    def degrid(side, lo, hi):
        def one(q):
            hot_row, hot_col = hots(vis_all[side, q], h, base, rows_own)
            val = jnp.dot(model[...], hot_col, preferred_element_type=f32)
            val = val[: 2 * rows_own] + val[2 * rows_own :]
            vr_ = jnp.sum(jnp.where(hot_row, val[:rows_own], 0.0), 0, keepdims=True)
            vi_ = jnp.sum(jnp.where(hot_row, val[rows_own:], 0.0), 0, keepdims=True)
            return jnp.concatenate([vr_, vi_], 0)

        def body(t, carry):
            a = one(lo + 2 * t)
            b = one(lo + 2 * t + 1)
            vals[side, lo + 2 * t] = a
            vals[side, lo + 2 * t + 1] = b
            return carry

        lax.fori_loop(0, (hi - lo) // 2, body, 0)

    def back(d, to, slot):
        return pltpu.make_async_remote_copy(
            vals.at[h, to], slots.at[slot], ws.at[d], wr.at[d],
            device_id=device(to, h), device_id_type=MESH,
        )

    stage_two(0)
    gridding(h, 0, half)
    stage_two(1)
    gridding(h, half, chips)
    stage_three(0)
    land(k_vis, vis_all.at[1 - h])
    gridding(1 - h, 0, half)
    stage_three(1)
    gridding(1 - h, half, chips)
    turn(0)
    turn(1)
    degrid(1 - h, 0, half)
    stage_five(0)
    degrid(1 - h, half, chips)
    k_vals = send(vals.at[1 - h], pair_vals, sib)
    stage_five(1)
    degrid(h, 0, half)
    stage_six(0)
    degrid(h, half, chips)
    stage_six(1)
    land(k_vals, pair_vals)
    vals[h] = vals[h] + pair_vals[...]
    peers(lambda d, to, frm: back(d, to, me).start())
    finish(0)
    finish(1)
    peers(lambda d, to, frm: back(d, to, frm).wait_recv())
    start = vals[h, me]
    res_ref[...] = obs_ref[...] - lax.fori_loop(
        1, chips, lambda d, t: t + slots[lax.rem(me + d, chips)], start
    )
    for k, index in cross:
        land(k, g_ref.at[(1 - h,) + index])
    for copy in sent:
        copy.wait_send()
    peers(lambda d, to, frm: link(d, to, me).wait_send())
    peers(lambda d, to, frm: back(d, to, me).wait_send())


def main(ro, co, sub, u, v, obs, facet, scale):
    _, _, nx, ny, nz = geometry()
    chips = nx * ny * nz
    fs = facet.shape[0]
    nv = obs.shape[1]
    rows_own = NR * SG // chips
    long = nz * rows_own
    copies = 128
    dma = pltpu.SemaphoreType.DMA
    return pl.pallas_call(
        functools.partial(main_kernel, scale),
        out_shape=[
            jax.ShapeDtypeStruct((2, 2, 2, nx, ny, long, SG // 2), bf16),
            jax.ShapeDtypeStruct((NR * SG, 2 * fs), bf16),
            jax.ShapeDtypeStruct((NR * SG, 2 * fs), bf16),
            jax.ShapeDtypeStruct((NC, 2 * SG, fs), bf16),
            jax.ShapeDtypeStruct((2, nv), f32),
        ],
        in_specs=[SM, SM] + [VM] * 5,
        out_specs=[VM] * 5,
        scratch_shapes=[
            pltpu.VMEM((SG, SG), bf16),
            pltpu.VMEM((SG, SG), bf16),
            pltpu.VMEM((SG, 2 * fs), bf16),
            pltpu.VMEM((SG, 2 * fs), bf16),
            pltpu.VMEM((4, nv), f32),
            pltpu.VMEM((2, chips, 4, nv), f32),
            pltpu.VMEM((fs, fs), bf16),
            pltpu.VMEM((2, 2, nx, ny, long, SG // 2), f32),
            pltpu.VMEM((2, 2, nx, ny, long, SG // 2), bf16),
            pltpu.VMEM((5 * rows_own, SG), f32),
            pltpu.VMEM((2, ny, long, SG // 2), f32),
            pltpu.VMEM((2, nx, long, SG // 2), f32),
            pltpu.VMEM((2, ny, long, SG // 2), bf16),
            pltpu.VMEM((2, nx, long, SG // 2), bf16),
            pltpu.VMEM((2, nx - 1, ny, long, SG // 2), bf16),
            pltpu.VMEM((2, ny - 1, nx, long, SG // 2), bf16),
            pltpu.VMEM((2, ny - 1, long, SG // 2), bf16),
            pltpu.VMEM((2, nx - 1, long, SG // 2), bf16),
            pltpu.VMEM((2, nz, rows_own, SG), f32),
            pltpu.VMEM((2, nz, rows_own, SG), bf16),
            pltpu.VMEM((2, nz - 1, rows_own, SG), bf16),
            pltpu.VMEM((2, nz, rows_own, SG), bf16),
            pltpu.VMEM((4 * rows_own, SG), bf16),
            pltpu.VMEM((2, chips, 2, nv), f32),
            pltpu.VMEM((chips, 2, nv), f32),
            pltpu.VMEM((chips, 2, nv), f32),
            dma((copies,)),
            dma((copies,)),
            dma((chips,)),
            dma((chips,)),
            dma((chips,)),
            dma((chips,)),
            dma,
        ],
        compiler_params=pltpu.CompilerParams(
            collective_id=0, has_side_effects=True, vmem_limit_bytes=LIMIT
        ),
        name="cycle",
    )(ro, co, sub, u, v, obs, facet)


def backward_kernel(scale, g_ref, ar_ref, ai_ref, bt_ref, image_ref):
    _, h, _, _ = position()
    fs = image_ref.shape[0]
    cut = pl.ds(pl.multiple_of(h * fs, fs), fs)
    first = (((0,), (0,)), ((), ()))
    g = jnp.concatenate([g_ref[c, w, p] for c in range(NC) for p in range(2) for w in range(2)], 1)
    one = lax.dot_general(ar_ref[:, cut], g, first, preferred_element_type=f32)
    two = lax.dot_general(ai_ref[:, cut], g, first, preferred_element_type=f32)
    parts = []
    for c in range(NC):
        re = slice(2 * c * SG, (2 * c + 1) * SG)
        im = slice((2 * c + 1) * SG, (2 * c + 2) * SG)
        parts += [one[:, re] + two[:, im], one[:, im] - two[:, re]]
    u = jnp.concatenate(parts, 1).astype(bf16)
    b = bt_ref[...].reshape(2 * NC * SG, fs)
    image_ref[...] = jnp.dot(u, b, preferred_element_type=f32) * scale


def backward(g, ar, ai, bt, scale):
    fs = bt.shape[2]
    return pl.pallas_call(
        functools.partial(backward_kernel, scale),
        out_shape=jax.ShapeDtypeStruct((fs, fs), f32),
        in_specs=[VM] * 4,
        out_specs=VM,
        compiler_params=pltpu.CompilerParams(vmem_limit_bytes=LIMIT),
        name="backward",
    )(g, ar, ai, bt)


def shards(facet_image, row_offsets, col_offsets, vis_subgrid, vis_u, vis_v, observed):
    rows, cols, _, _, _ = geometry()
    fs = facet_image.shape[0]
    scale_in = 1.0 / (fs * math.sqrt(rows * cols))
    scale_out = 1.0 / (SG * math.sqrt(NR * NC))
    g, ar, ai, bt, residual = main(
        row_offsets, col_offsets, vis_subgrid[None], vis_u[None], vis_v[None],
        observed, facet_image, scale_in / SG,
    )
    image = backward(g.reshape(NC, 2, 2, NR * SG, SG // 2), ar, ai, bt, scale_out / SG)
    return (image, residual)


def solution(mesh):
    in_specs = (
        P("frow", "fcol"),
        P(),
        P(),
        P(("frow", "fcol")),
        P(("frow", "fcol")),
        P(("frow", "fcol")),
        P(None, ("frow", "fcol")),
    )
    out_specs = (P("frow", "fcol"), P(None, ("frow", "fcol")))
    return jax.shard_map(shards, mesh=mesh, in_specs=in_specs, out_specs=out_specs, check_vma=False)
```

profile of v0, /device:TPU:0, one launch (start us, length us, event | category | flops | bytes accessed | tf_op | source)
XLA Modules:
  0.0 46.9 jit_solution(14337284443446923350)
XLA Ops:
  0.6 40.6 %cycle.1 = (bf16[2,2,2,2,2,128,128]{6,5,4,3,2,1,0:T(8,128)(2,1)}, bf16[512,1024]{1,0:T(8,128)(2,1)}, bf16[512,1024]{1,0:T(8,128)(2,1)}, bf16[2,512,512]{2,1,0:T(8,128)(2,1)}, f32[2,512]{1,0:T(2,128)}) custom-call(s32[2]{0:T(128)} %ro_ref.1, s32[2]{0:T(128)} %co_ref.1, s32[1,512]{1,0:T(1,128)} %bitcast.5, s32[1,512]{1,0:T(1,128)} %bitcast.6, ...), custom_call_target="tpu_custom_call" | custom-call | tf_op jit(solution)/shard_map/cycle/pallas_call | solution.py:428
  41.3 0.0 copy-start
  41.3 5.0 %backward.1 = f32[512,512]{1,0:T(8,128)} custom-call(bf16[2,2,2,512,128]{4,3,2,1,0:T(8,128)(2,1)} %bitcast.4, bf16[512,1024]{1,0:T(8,128)(2,1)} %get-tuple-element.8.ar_ref, bf16[512,1024]{1,0:T(8,128)(2,1)} %get-tuple-element.9.ai_ref, bf16[2,512,512]{2,1,0:T(8,128)(2,1)} %get-tuple-element.10.bt_ref), custom_call_target="tpu_custom_call" | custom-call | tf_op jit(solution)/shard_map/backward/pallas_call | solution.py:501
  46.3 0.0 copy-done
  46.3 0.6 %copy.10 = f32[2,512]{1,0:T(2,128)} copy(f32[2,512]{1,0:T(2,128)S(1)} %copy-done) | data formatting | bytes 8192
Async XLA Ops:
  41.3 5.0 %copy-start = (f32[2,512]{1,0:T(2,128)S(1)}, f32[2,512]{1,0:T(2,128)}, u32[]{:S(2)}) copy-start(f32[2,512]{1,0:T(2,128)} %get-tuple-element.15) | copy-start | bytes 12292
where the time goes:
time: 47 us; the launch traced here: 46.9 us
  Pallas kernels  45.6 us (97%)
  between operations  0.65 us (1%)
  local copies, waits for them, and re-layouts  0.6 us (1%)
    pallas_call x1, Pallas kernels, main(): pl.pallas_call(functools.partial(main_kernel, scale), out_shape=[jax.Shap...  40.6 us
    pallas_call x1, Pallas kernels, backward(): pl.pallas_call(functools.partial(backward_kernel, scale), out_shape=jax.S...  4.99 us

commit v1 on v0

--- a/solution.py
+++ b/solution.py
@@ -18,7 +18,7 @@
 MESH = pl.DeviceIdType.MESH
 VM = pl.BlockSpec(memory_space=pltpu.VMEM)
 SM = pl.BlockSpec(memory_space=pltpu.SMEM)
-LIMIT = 60 << 20
+LIMIT = 24 << 20
 
 
 def geometry():

time: 47 us -> 46.1 us (0.981)
  Pallas kernels: 45.6 us -> 40.9 us
  local copies, waits for them, and re-layouts: 0.6 us -> 4.35 us
    unnamed x3 -> x15, local copies, waits for them, and re-layouts: 0.6 us -> 4.35 us
    pallas_call x1, Pallas kernels: 40.6 us -> 38 us  [main(): pl.pallas_call(functools.partial(main_kernel, scale), out_shape=[jax.Shap...]
    pallas_call x1, Pallas kernels: 4.99 us -> 2.83 us  [backward(): pl.pallas_call(functools.partial(backward_kernel, scale), out_shape=jax.S...]
where the time goes in v1:
time: 46.1 us; the launch traced here: 45.9 us
  Pallas kernels  40.9 us (89%)
  local copies, waits for them, and re-layouts  4.35 us (9%)
  between operations  0.67 us (1%)
    pallas_call x1, Pallas kernels, main(): pl.pallas_call(functools.partial(main_kernel, scale), out_shape=[jax.Shap...  38 us
    unnamed x15, local copies, waits for them, and re-layouts  4.35 us
    pallas_call x1, Pallas kernels, backward(): pl.pallas_call(functools.partial(backward_kernel, scale), out_shape=jax.S...  2.83 us

profile of v1, /device:TPU:0, one launch (start us, length us, event | category | flops | bytes accessed | tf_op | source)
XLA Modules:
  0.0 45.9 jit_solution(5981338616687848049)
XLA Ops:
  0.6 0.0 copy-start.1
  0.6 0.0 copy-start.5
  0.7 0.0 copy-start.6
  0.7 0.7 %copy-done.1 = f32[2,512]{1,0:T(2,128)S(1)} copy-done((f32[2,512]{1,0:T(2,128)S(1)}, f32[2,512]{1,0:T(2,128)}, u32[]{:S(2)}) %copy-start.1) | copy-done | bytes 4120
  1.3 0.0 copy-done.5
  1.3 0.0 copy-done.6
  1.3 0.0 copy-start
  1.3 1.0 %copy-done = bf16[512,512]{1,0:T(8,128)(2,1)S(1)} copy-done((bf16[512,512]{1,0:T(8,128)(2,1)S(1)}, bf16[512,512]{1,0:T(8,128)(2,1)}, u32[]{:S(2)}) %copy-start) | copy-done | bytes 524312
  2.4 0.0 copy-start.2
  2.4 0.7 %copy-done.2 = s32[512]{0:T(512)S(1)} copy-done((s32[512]{0:T(512)S(1)}, s32[512]{0:T(512)}, u32[]{:S(2)}) %copy-start.2) | copy-done | bytes 2072
  3.1 0.0 copy-start.3
  3.1 0.7 %copy-done.3 = s32[512]{0:T(512)S(1)} copy-done((s32[512]{0:T(512)S(1)}, s32[512]{0:T(512)}, u32[]{:S(2)}) %copy-start.3) | copy-done | bytes 2072
  3.7 0.0 copy-start.4
  3.7 0.7 %copy-done.4 = s32[512]{0:T(512)S(1)} copy-done((s32[512]{0:T(512)S(1)}, s32[512]{0:T(512)}, u32[]{:S(2)}) %copy-start.4) | copy-done | bytes 2072
  4.4 38.0 %cycle.1 = (bf16[2,2,2,2,2,128,128]{6,5,4,3,2,1,0:T(8,128)(2,1)S(1)}, bf16[512,1024]{1,0:T(8,128)(2,1)S(1)}, bf16[512,1024]{1,0:T(8,128)(2,1)S(1)}, bf16[2,512,512]{2,1,0:T(8,128)(2,1)S(1)}, f32[2,512]{1,0:T(2,128)S(1)}) custom-call(s32[2]{0:T(128)S(1)} %copy-done.5, s32[2]{0:T(128)S(1)} %copy-done.6, s32[1,512]{1,0:T(1,128)S(1)} %bitcast.5, ...), custom_call_target="tpu_custom_call" | custom-call | tf_op jit(solution)/shard_map/cycle/pallas_call | solution.py:428
  42.5 2.8 %backward.1 = f32[512,512]{1,0:T(8,128)} custom-call(bf16[2,2,2,512,128]{4,3,2,1,0:T(8,128)(2,1)S(1)} %bitcast.4, bf16[512,1024]{1,0:T(8,128)(2,1)S(1)} %get-tuple-element.8.ar_ref, bf16[512,1024]{1,0:T(8,128)(2,1)S(1)} %get-tuple-element.9.ai_ref, bf16[2,512,512]{2,1,0:T(8,128)(2,1)S(1)} %get-tuple-element.10.bt_ref), custom_call_target="tpu_custom_call" | custom-call | tf_op jit(solution)/shard_map/backward/pallas_call | solution.py:501
  45.3 0.6 %copy.10 = f32[2,512]{1,0:T(2,128)} copy(f32[2,512]{1,0:T(2,128)S(1)} %get-tuple-element.15) | data formatting | bytes 8192
Async XLA Ops:
  0.6 0.7 %copy-start.1 = (f32[2,512]{1,0:T(2,128)S(1)}, f32[2,512]{1,0:T(2,128)}, u32[]{:S(2)}) copy-start(f32[2,512]{1,0:T(2,128)} %obs_ref.1) | copy-start | bytes 12292
  0.6 0.7 %copy-start.5 = (s32[2]{0:T(128)S(1)}, s32[2]{0:T(128)}, u32[]{:S(2)}) copy-start(s32[2]{0:T(128)} %ro_ref.1) | copy-start | bytes 28
  0.7 0.7 %copy-start.6 = (s32[2]{0:T(128)S(1)}, s32[2]{0:T(128)}, u32[]{:S(2)}) copy-start(s32[2]{0:T(128)} %co_ref.1) | copy-start | bytes 28
  1.3 1.0 %copy-start = (bf16[512,512]{1,0:T(8,128)(2,1)S(1)}, bf16[512,512]{1,0:T(8,128)(2,1)}, u32[]{:S(2)}) copy-start(bf16[512,512]{1,0:T(8,128)(2,1)} %facet_ref.1) | copy-start | bytes 1572868
  2.4 0.7 %copy-start.2 = (s32[512]{0:T(512)S(1)}, s32[512]{0:T(512)}, u32[]{:S(2)}) copy-start(s32[512]{0:T(512)} %param.10) | copy-start | bytes 6148
  3.1 0.7 %copy-start.3 = (s32[512]{0:T(512)S(1)}, s32[512]{0:T(512)}, u32[]{:S(2)}) copy-start(s32[512]{0:T(512)} %param.11) | copy-start | bytes 6148
  3.7 0.7 %copy-start.4 = (s32[512]{0:T(512)S(1)}, s32[512]{0:T(512)}, u32[]{:S(2)}) copy-start(s32[512]{0:T(512)} %param.12) | copy-start | bytes 6148

commit v2 on v1

v2 whole, which is shorter than its diff:
```python
import functools
import math

import jax
import jax.numpy as jnp
from jax import lax
from jax.experimental import pallas as pl
from jax.experimental.pallas import tpu as pltpu
from jax.sharding import PartitionSpec as P

SKY = 65536
SG = 256
NR = 2
NC = 2
f32 = jnp.float32
bf16 = jnp.bfloat16
i32 = jnp.int32
MESH = pl.DeviceIdType.MESH
VM = pl.BlockSpec(memory_space=pltpu.VMEM)
HB = pl.BlockSpec(memory_space=pltpu.HBM)
LIMIT = 32 << 20


scope = jax.named_scope


def geometry():
    rows = lax.axis_size("frow")
    cols = lax.axis_size("fcol")
    nx = rows // 2
    ny = 1 << ((cols.bit_length() - 1) // 2)
    nz = cols // ny
    return rows, cols, nx, ny, nz


def position():
    _, _, _, ny, _ = geometry()
    frow = lax.axis_index("frow")
    fcol = lax.axis_index("fcol")
    return frow // 2, frow % 2, fcol % ny, fcol // ny


def phase(product):
    angle = (product & (SKY - 1)).astype(f32) * (2.0 * math.pi / SKY)
    return jnp.cos(angle), jnp.sin(angle)


def expand(first, places, c_ref, s_ref):
    n = places.shape[1]
    steps = lax.broadcasted_iota(i32, (16, n), 0)
    c0, s0 = phase(steps * places)
    c1, s1 = phase((first + 16 * steps) * places)
    for k in range(SG // 16):
        ck = c1[k : k + 1]
        sk = s1[k : k + 1]
        c_ref[k * 16 : k * 16 + 16, :] = (ck * c0 - sk * s0).astype(bf16)
        s_ref[k * 16 : k * 16 + 16, :] = (sk * c0 + ck * s0).astype(bf16)


def place(q):
    _, _, _, ny, nz = geometry()
    return lax.div(q, ny * nz), lax.rem(lax.div(q, nz), ny), lax.rem(q, nz)


def device(q, h):
    _, _, _, ny, _ = geometry()
    x, y, z = place(q)
    return (2 * x + h, z * ny + y)


def hots(vis, h, owned):
    n = vis.shape[1]
    cell = vis[0:1].astype(i32)
    sub = cell // (SG * SG)
    row = (sub // NC) * SG + (cell // SG) % SG
    row = jnp.where(sub % NC == h, row, -1)
    hot_col = lax.broadcasted_iota(i32, (SG, n), 0) == cell % SG
    return owned == row, jnp.where(hot_col, 1.0, 0.0).astype(bf16)


def semaphores():
    plan = {}
    total = 0
    for at, kind in enumerate((
        "xa", "yb", "ya", "xb", "z", "back_z", "back_ya", "back_xb", "back_xa", "back_yb", "cross",
        "facet", "vis", "cells", "values", "answers",
    )):
        count = 4 if at < 11 else 1
        plan[kind] = (at, total, count)
        total += count
    return plan, total


def main_kernel(
    scale, facet_hbm, ro_hbm, co_hbm, sub_hbm, u_hbm, v_hbm, obs_hbm,
    acc_ref, last_ref, bt_ref, res_ref,
    facet_ref, ro_ref, co_ref, sub_ref, u_ref, v_ref, obs_ref,
    kk, ks, rc, rs, a_tab, p_ref, vis_ref, vis_all, other, z_ref, zb_ref, g_ref, grid_acc,
    acc_a, acc_b, send_a, send_b, got_a1, got_b1, got_a2, got_b2,
    own_z, send_z, got_z, gz, model, vals, pair_vals, slots,
    ssem, rsem, lsem,
):
    rows, cols, nx, ny, nz = geometry()
    x, h, y, z = position()
    chips = nx * ny * nz
    me = (x * ny + y) * nz + z
    fs = facet_ref.shape[0]
    nv = vis_ref.shape[1]
    rows_own = NR * SG // chips
    hr = rows_own // 2
    hlong = nz * hr
    part = 2 * hlong
    wide = SG // 2
    waves = range(4)
    sib = (2 * x + 1 - h, lax.axis_index("fcol"))
    barrier = pltpu.get_barrier_semaphore()

    def peers(act):
        def step(d, carry):
            act(d, lax.rem(me + d, chips), lax.rem(me - d + chips, chips))
            return carry

        lax.fori_loop(1, chips, step, 0)

    peers(lambda d, to, frm: pl.semaphore_signal(barrier, inc=1, device_id=device(to, h), device_id_type=MESH))
    pl.semaphore_signal(barrier, inc=1, device_id=sib, device_id_type=MESH)
    loads = []
    for k, (src, dst) in enumerate((
        (ro_hbm, ro_ref), (co_hbm, co_ref), (sub_hbm, sub_ref), (u_hbm, u_ref), (v_hbm, v_ref),
        (obs_hbm, obs_ref), (facet_hbm, facet_ref),
    )):
        loads.append(pltpu.make_async_copy(src, dst, lsem.at[k]))
        loads[-1].start()
    plan = semaphores()[0]

    def send(kind, w, src, dst, to):
        at, base, _ = plan[kind]
        pltpu.make_async_remote_copy(
            src, dst, ssem.at[at], rsem.at[base + w], device_id=to, device_id_type=MESH
        ).start()

    def land(kind, w, like):
        at, base, _ = plan[kind]
        pltpu.make_async_remote_copy(
            like, like, ssem.at[at], rsem.at[base + w], device_id=sib, device_id_type=MESH
        ).wait_recv()

    def sentall(kind, like):
        at, base, _ = plan[kind]
        pltpu.make_async_remote_copy(
            like, like, ssem.at[at], rsem.at[base], device_id=sib, device_id_type=MESH
        ).wait_send()

    with scope("expandK"):
        expand(0, lax.broadcasted_iota(i32, (1, SG), 1) * (SKY // SG), kk, ks)
    kcos = kk[...]
    ksin = ks[...]

    def compose(n, start, unit):
        places = (start + lax.broadcasted_iota(i32, (1, n), 1)) * unit
        expand(0, places, rc.at[:, :n], rs.at[:, :n])
        c = rc[:, :n]
        s = rs[:, :n]
        re = jnp.dot(kcos, c, preferred_element_type=f32) + jnp.dot(ksin, s, preferred_element_type=f32)
        im = jnp.dot(ksin, c, preferred_element_type=f32) - jnp.dot(kcos, s, preferred_element_type=f32)

        def shifted(offset):
            cos, sin = phase(offset * places)
            return (re * cos + im * sin).astype(bf16), (im * cos - re * sin).astype(bf16)

        return shifted

    with scope("composeB"):
        shifted = compose(fs, lax.axis_index("fcol") * fs, SKY // (cols * fs))
        loads[0].wait()
        loads[1].wait()
        for c in range(NC):
            re, im = shifted(co_ref[c])
            for q in range(2):
                bt_ref[c, q, :wide] = re[q * wide : (q + 1) * wide]
                bt_ref[c, q, wide:] = im[q * wide : (q + 1) * wide]
    with scope("cells"):
        for copy in loads[2:6]:
            copy.wait()
        cell = (sub_ref[...] * SG + u_ref[...]) * SG + v_ref[...]
        vis_ref[0:1] = cell.astype(f32)
        vis_ref[1:3] = obs_ref[...]
        vis_ref[3:4] = jnp.zeros((1, nv), f32)
        mine = pltpu.make_async_copy(vis_ref, vis_all.at[h, me], lsem.at[7])
        mine.start()
    with scope("barwait"):
        pl.semaphore_wait(barrier, chips)
    send("facet", 0, facet_hbm, other, sib)
    peers(lambda d, to, frm: send("cells", 0, vis_ref, vis_all.at[h, me], device(to, h)))
    with scope("composeA"):
        shifted = compose(2 * fs, x * (2 * fs), SKY // (rows * fs))
        for r in range(NR):
            pair = shifted(ro_ref[r])
            for b in range(SG // part):
                blk = r * (SG // part) + b
                for e in range(2):
                    for p in range(2):
                        cut = slice(b * part + e * hlong, b * part + (e + 1) * hlong)
                        a_tab[p, e, blk * hlong : (blk + 1) * hlong] = pair[p][cut]

    mine.wait()
    loads[6].wait()

    def project(ref, q):
        return lax.dot_general(
            ref[...], bt_ref[h, q], (((1,), (1,)), ((), ())), preferred_element_type=f32
        ).astype(bf16)

    own_cut = pl.ds(pl.multiple_of(h * fs, fs), fs)
    other_cut = pl.ds(pl.multiple_of((1 - h) * fs, fs), fs)

    def to_x(d):
        return device((lax.rem(x + d, nx) * ny + y) * nz + z, h)

    def to_y(d):
        return device((x * ny + lax.rem(y + d, ny)) * nz + z, h)

    def to_z(d):
        return device((x * ny + y) * nz + lax.rem(z + d, nz), h)

    def produce(w):
        q, e = w // 2, w % 2
        if e == 0:
            p_ref[own_cut] = project(facet_ref, q)
            if q == 0:
                land("facet", 0, other)
            p_ref[other_cut] = project(other, q)
        both = jnp.dot(a_tab[:, e].reshape(2 * nx * ny * hlong, 2 * fs), p_ref[...], preferred_element_type=f32)
        one = both[: nx * ny * hlong]
        two = both[nx * ny * hlong :]
        zr = (one[:, :wide] - two[:, wide:]).reshape(nx, ny, hlong, wide)
        zi = (one[:, wide:] + two[:, :wide]).reshape(nx, ny, hlong, wide)
        z_ref[w, 0] = zr
        z_ref[w, 1] = zi
        zb_ref[w, 0] = zr.astype(bf16)
        zb_ref[w, 1] = zi.astype(bf16)
        for d in range(1, nx):
            send("xa", w, zb_ref.at[w, 0, lax.rem(x + d, nx)], got_a1.at[w, d - 1], to_x(d))
        for d in range(1, ny):
            send("yb", w, zb_ref.at[w, 1, :, lax.rem(y + d, ny)], got_b1.at[w, d - 1], to_y(d))

    owned_row = lax.broadcasted_iota(i32, (rows_own, nv), 0)
    owned_row = (x * ny + y) * part + z * hr + (owned_row // hr) * hlong + owned_row % hr

    def gridding(side, lo, hi):
        def one(q):
            vis = vis_all[side, q]
            hot_row, hot_col = hots(vis, h, owned_row)
            parts = [vis[1:2], vis[2:3], jnp.ones_like(vis[0:1])]
            left = jnp.concatenate([jnp.where(hot_row, t, 0.0) for t in parts], 0).astype(bf16)
            return lax.dot_general(left, hot_col, (((1,), (1,)), ((), ())), preferred_element_type=f32)

        def body(t, carry):
            got = one(lo + 2 * t) + one(lo + 2 * t + 1)
            grid_acc[...] += got
            return carry

        lax.fori_loop(0, (hi - lo) // 2, body, 0)

    def stage_two(w):
        land("xa", w, got_a1.at[w])
        total = z_ref[w, 0, x]
        for d in range(nx - 1):
            total = total + got_a1[w, d].astype(f32)
        acc_a[w] = total
        send_a[w] = total.astype(bf16)
        for d in range(1, ny):
            send("ya", w, send_a.at[w, lax.rem(y + d, ny)], got_a2.at[w, d - 1], to_y(d))
        land("yb", w, got_b1.at[w])
        total = z_ref[w, 1, :, y]
        for d in range(ny - 1):
            total = total + got_b1[w, d].astype(f32)
        acc_b[w] = total
        send_b[w] = total.astype(bf16)
        for d in range(1, nx):
            send("xb", w, send_b.at[w, lax.rem(x + d, nx)], got_b2.at[w, d - 1], to_x(d))

    def stage_three(w):
        land("ya", w, got_a2.at[w])
        re = acc_a[w, y]
        for d in range(ny - 1):
            re = re + got_a2[w, d].astype(f32)
        land("xb", w, got_b2.at[w])
        im = acc_b[w, x]
        for d in range(nx - 1):
            im = im + got_b2[w, d].astype(f32)
        for k in range(nz):
            cut = slice(k * hr, (k + 1) * hr)
            own_z[w, k, :, :wide] = re[cut]
            own_z[w, k, :, wide:] = im[cut]
            send_z[w, k, :, :wide] = re[cut].astype(bf16)
            send_z[w, k, :, wide:] = im[cut].astype(bf16)
        for d in range(1, nz):
            send("z", w, send_z.at[w, lax.rem(z + d, nz)], got_z.at[w, d - 1], to_z(d))

    def turn(w):
        q, e = w // 2, w % 2
        land("z", w, got_z.at[w])
        total = own_z[w, z]
        for d in range(nz - 1):
            total = total + got_z[w, d].astype(f32)
        m = total * scale
        cut = slice(q * wide, (q + 1) * wide)
        got = [grid_acc[p * rows_own + e * hr : p * rows_own + (e + 1) * hr, cut] for p in range(3)]
        hat_re = got[0] - got[2] * m[:, :wide]
        hat_im = got[1] - got[2] * m[:, wide:]
        gz[w, z, :, :wide] = hat_re.astype(bf16)
        gz[w, z, :, wide:] = hat_im.astype(bf16)
        for d in range(1, nz):
            send("back_z", w, gz.at[w, z], gz.at[w, z], to_z(d))
        model[e * hr : (e + 1) * hr, cut] = m[:, :wide]
        model[rows_own + e * hr : rows_own + (e + 1) * hr, cut] = m[:, wide:]

    def over(w, index):
        src = g_ref.at[(h, w) + index]
        send("cross", w, src, src, sib)

    def stage_five(w):
        land("back_z", w, gz.at[w, : nz - 1])
        for k in range(nz):
            cut = slice(k * hr, (k + 1) * hr)
            g_ref[h, w, 0, x, y, cut, :] = gz[w, k, :, :wide]
            g_ref[h, w, 1, x, y, cut, :] = gz[w, k, :, wide:]
        for d in range(1, ny):
            blk = g_ref.at[h, w, 0, x, y]
            send("back_ya", w, blk, blk, to_y(d))
        for d in range(1, nx):
            blk = g_ref.at[h, w, 1, x, y]
            send("back_xb", w, blk, blk, to_x(d))
        over(w, (0, x, y))
        over(w, (1, x, y))

    def stage_six(w):
        land("back_ya", w, g_ref.at[h, w, 0, x, : ny - 1])
        for d in range(1, nx):
            blk = g_ref.at[h, w, 0, x]
            send("back_xa", w, blk, blk, to_x(d))
        land("back_xb", w, g_ref.at[h, w, 1, : nx - 1, y])
        for d in range(1, ny):
            blk = g_ref.at[h, w, 1, :, y]
            send("back_yb", w, blk, blk, to_y(d))
        for d in range(1, ny):
            over(w, (0, x, lax.rem(y - d + ny, ny)))
        for d in range(1, nx):
            over(w, (1, lax.rem(x - d + nx, nx), y))

    def finish(w):
        land("back_xa", w, g_ref.at[h, w, 0, : nx - 1])
        for d in range(1, nx):
            over(w, (0, lax.rem(x - d + nx, nx)))
        land("back_yb", w, g_ref.at[h, w, 1, :, : ny - 1])
        for d in range(1, ny):
            over(w, (1, slice(None), lax.rem(y - d + ny, ny)))

    def crossed(w):
        land("cross", w, g_ref.at[1 - h, w])

    def degrid(side, lo, hi):
        m = model[...].astype(bf16)

        def one(q):
            hot_row, hot_col = hots(vis_all[side, q], h, owned_row)
            val = jnp.dot(m, hot_col, preferred_element_type=f32)
            vr_ = jnp.sum(jnp.where(hot_row, val[:rows_own], 0.0), 0, keepdims=True)
            vi_ = jnp.sum(jnp.where(hot_row, val[rows_own:], 0.0), 0, keepdims=True)
            return jnp.concatenate([vr_, vi_], 0)

        def body(t, carry):
            a = one(lo + 2 * t)
            b = one(lo + 2 * t + 1)
            vals[side, lo + 2 * t] = a
            vals[side, lo + 2 * t + 1] = b
            return carry

        lax.fori_loop(0, (hi - lo) // 2, body, 0)

    first = (((0,), (0,)), ((), ()))
    tall = 2 * nx * ny * hlong

    def spread(c, q):
        g = [
            jnp.concatenate([g_ref[c, 2 * q + e, p].reshape(tall // 2, wide) for e in range(2)], 0)
            for p in range(2)
        ]
        g = jnp.concatenate(g, 1)
        one = lax.dot_general(a_tab[0, :, :, own_cut].reshape(tall, fs), g, first, preferred_element_type=f32)
        two = lax.dot_general(a_tab[1, :, :, own_cut].reshape(tall, fs), g, first, preferred_element_type=f32)
        return jnp.concatenate([one[:, :wide] + two[:, wide:], one[:, wide:] - two[:, :wide]], 1).astype(bf16)

    def image(c, q):
        return jnp.dot(spread(c, q), bt_ref[c, q], preferred_element_type=f32)

    grid_acc[...] = jnp.zeros_like(grid_acc)
    half = chips // 2
    quarter = chips // 4
    seen = [0]

    def grid(n=quarter):
        lo = seen[0]
        seen[0] = lo + n
        side, at = lo // chips, lo % chips
        if side == 1 and at == 0:
            land("vis", 0, vis_all.at[1 - h])
        with scope("grid%d" % lo):
            gridding(h if side == 0 else 1 - h, at, at + n)

    def run(name, w):
        with scope("%s%d" % (name.__name__, w)):
            name(w)

    run(produce, 0)
    run(produce, 1)
    run(produce, 2)
    run(produce, 3)
    with scope("viswait"):
        land("cells", 0, vis_all.at[h, : chips - 1])
    send("vis", 0, vis_all.at[h], vis_all.at[h], sib)
    run(stage_two, 0)
    run(stage_two, 1)
    grid()
    run(stage_two, 2)
    run(stage_three, 0)
    run(stage_two, 3)
    run(stage_three, 1)
    grid()
    grid()
    run(stage_three, 2)
    grid()
    run(stage_three, 3)
    grid()
    grid()
    grid()
    grid()
    run(turn, 0)
    run(turn, 1)
    run(turn, 2)
    run(turn, 3)
    with scope("degrid0"):
        degrid(1 - h, 0, half)
    run(stage_five, 0)
    run(stage_five, 1)
    with scope("degrid1"):
        degrid(1 - h, half, chips)
    send("values", 0, vals.at[1 - h], pair_vals, sib)
    run(stage_five, 2)
    run(stage_six, 0)
    run(stage_five, 3)
    run(stage_six, 1)
    with scope("degrid2"):
        degrid(h, 0, half)
    run(stage_six, 2)
    run(finish, 0)
    run(stage_six, 3)
    run(finish, 1)
    with scope("degrid3"):
        degrid(h, half, chips)
    with scope("landvals"):
        land("values", 0, pair_vals)
        vals[h] = vals[h] + pair_vals[...]
    with scope("backstart"):
        peers(lambda d, to, frm: send("answers", 0, vals.at[h, to], slots.at[me], device(to, h)))
    with scope("imageown0"):
        acc_ref[...] = image(h, 0)
    run(finish, 2)
    run(crossed, 0)
    run(crossed, 1)
    run(finish, 3)
    with scope("imageother0"):
        acc_ref[...] += image(1 - h, 0)
    with scope("imageown1"):
        acc_ref[...] += image(h, 1)
    with scope("backwait"):
        land("answers", 0, slots.at[: chips - 1])
    with scope("result"):
        start = vals[h, me]
        res_ref[...] = obs_ref[...] - lax.fori_loop(
            1, chips, lambda d, t: t + slots[lax.rem(me + d, chips)], start
        )
    run(crossed, 2)
    run(crossed, 3)
    with scope("last"):
        last_ref[...] = spread(1 - h, 1)
    with scope("drain"):
        for kind, like in (
            ("xa", got_a1), ("yb", got_b1), ("ya", got_a2), ("xb", got_b2), ("z", got_z),
            ("back_z", got_z), ("back_ya", got_a2), ("back_xb", got_b2), ("back_xa", got_a1),
            ("back_yb", got_b1), ("cross", g_ref.at[h]), ("facet", other), ("vis", vis_all.at[h]),
            ("cells", vis_all.at[h, : chips - 1]), ("values", pair_vals),
            ("answers", slots.at[: chips - 1]),
        ):
            sentall(kind, like)


def main(ro, co, sub, u, v, obs, facet, scale):
    _, _, nx, ny, nz = geometry()
    chips = nx * ny * nz
    fs = facet.shape[0]
    nv = obs.shape[1]
    rows_own = NR * SG // chips
    hr = rows_own // 2
    hlong = nz * hr
    wide = SG // 2
    plan, total = semaphores()
    dma = pltpu.SemaphoreType.DMA
    return pl.pallas_call(
        functools.partial(main_kernel, scale),
        out_shape=[
            jax.ShapeDtypeStruct((fs, fs), f32),
            jax.ShapeDtypeStruct((fs, SG), bf16),
            jax.ShapeDtypeStruct((NC, 2, SG, fs), bf16),
            jax.ShapeDtypeStruct((2, nv), f32),
        ],
        in_specs=[HB] * 7,
        out_specs=[VM] * 4,
        scratch_shapes=[
            pltpu.VMEM((fs, fs), bf16),
            pltpu.SMEM((NR,), i32),
            pltpu.SMEM((NC,), i32),
            pltpu.VMEM((1, nv), i32),
            pltpu.VMEM((1, nv), i32),
            pltpu.VMEM((1, nv), i32),
            pltpu.VMEM((2, nv), f32),
            pltpu.VMEM((SG, SG), bf16),
            pltpu.VMEM((SG, SG), bf16),
            pltpu.VMEM((SG, 2 * fs), bf16),
            pltpu.VMEM((SG, 2 * fs), bf16),
            pltpu.VMEM((2, 2, nx * ny * hlong, 2 * fs), bf16),
            pltpu.VMEM((2 * fs, SG), bf16),
            pltpu.VMEM((4, nv), f32),
            pltpu.VMEM((2, chips, 4, nv), f32),
            pltpu.VMEM((fs, fs), bf16),
            pltpu.VMEM((4, 2, nx, ny, hlong, wide), f32),
            pltpu.VMEM((4, 2, nx, ny, hlong, wide), bf16),
            pltpu.VMEM((2, 4, 2, nx, ny, hlong, wide), bf16),
            pltpu.VMEM((3 * rows_own, SG), f32),
            pltpu.VMEM((4, ny, hlong, wide), f32),
            pltpu.VMEM((4, nx, hlong, wide), f32),
            pltpu.VMEM((4, ny, hlong, wide), bf16),
            pltpu.VMEM((4, nx, hlong, wide), bf16),
            pltpu.VMEM((4, nx - 1, ny, hlong, wide), bf16),
            pltpu.VMEM((4, ny - 1, nx, hlong, wide), bf16),
            pltpu.VMEM((4, ny - 1, hlong, wide), bf16),
            pltpu.VMEM((4, nx - 1, hlong, wide), bf16),
            pltpu.VMEM((4, nz, hr, SG), f32),
            pltpu.VMEM((4, nz, hr, SG), bf16),
            pltpu.VMEM((4, nz - 1, hr, SG), bf16),
            pltpu.VMEM((4, nz, hr, SG), bf16),
            pltpu.VMEM((2 * rows_own, SG), f32),
            pltpu.VMEM((2, chips, 2, nv), f32),
            pltpu.VMEM((chips, 2, nv), f32),
            pltpu.VMEM((chips, 2, nv), f32),
            dma((len(plan),)),
            dma((total,)),
            dma((8,)),
        ],
        compiler_params=pltpu.CompilerParams(
            collective_id=0, has_side_effects=True, vmem_limit_bytes=LIMIT
        ),
        name="cycle",
    )(*(pltpu.with_memory_space_constraint(a, pltpu.HBM) for a in (facet, ro, co, sub, u, v, obs)))


def finish_kernel(scale, acc_ref, last_ref, bt_ref, res_ref, image_hbm, out_hbm, buf, sem):
    _, h, _, _ = position()
    fs = acc_ref.shape[0]
    pieces = 4
    step = fs // pieces
    copies = [pltpu.make_async_copy(res_ref, out_hbm, sem.at[pieces])]
    copies[0].start()
    b = bt_ref[1 - h, 1]
    for k in range(pieces):
        cut = slice(k * step, (k + 1) * step)
        buf[cut] = (acc_ref[cut] + jnp.dot(last_ref[cut], b, preferred_element_type=f32)) * scale
        copies.append(pltpu.make_async_copy(buf.at[cut], image_hbm.at[cut], sem.at[k]))
        copies[-1].start()
    for copy in copies:
        copy.wait()


def finish(acc, last, bt, res, scale):
    fs = acc.shape[0]
    return pl.pallas_call(
        functools.partial(finish_kernel, scale),
        out_shape=[jax.ShapeDtypeStruct((fs, fs), f32), jax.ShapeDtypeStruct(res.shape, f32)],
        in_specs=[VM] * 4,
        out_specs=[HB] * 2,
        scratch_shapes=[pltpu.VMEM((fs, fs), f32), pltpu.SemaphoreType.DMA((5,))],
        compiler_params=pltpu.CompilerParams(vmem_limit_bytes=4 << 20),
        name="finish",
    )(acc, last, bt, res)


def shards(facet_image, row_offsets, col_offsets, vis_subgrid, vis_u, vis_v, observed):
    rows, cols, _, _, _ = geometry()
    fs = facet_image.shape[0]
    scale_in = 1.0 / (fs * math.sqrt(rows * cols))
    scale_out = 1.0 / (SG * math.sqrt(NR * NC))
    acc, last, bt, residual = main(
        row_offsets, col_offsets, vis_subgrid[None], vis_u[None], vis_v[None],
        observed, facet_image, scale_in / SG,
    )
    return tuple(finish(acc, last, bt, residual, scale_out / SG))


def solution(mesh):
    in_specs = (
        P("frow", "fcol"),
        P(),
        P(),
        P(("frow", "fcol")),
        P(("frow", "fcol")),
        P(("frow", "fcol")),
        P(None, ("frow", "fcol")),
    )
    out_specs = (P("frow", "fcol"), P(None, ("frow", "fcol")))
    return jax.shard_map(shards, mesh=mesh, in_specs=in_specs, out_specs=out_specs, check_vma=False)
```

time: 46.1 us -> 40.7 us (0.88)
  local copies, waits for them, and re-layouts: 4.35 us -> 0 us
  Pallas kernels: 40.9 us -> 39.9 us
    unnamed x15 -> x0, local copies, waits for them, and re-layouts: 4.35 us -> none
    pallas_call x1, Pallas kernels: 2.83 us -> 1.23 us  [finish(): pl.pallas_call(functools.partial(finish_kernel, scale), out_shape=[jax.Sh...]
    pallas_call x1, Pallas kernels: 38 us -> 38.7 us  [main(): pl.pallas_call(functools.partial(main_kernel, scale), out_shape=[jax.Shap...]
where the time goes in v2:
time: 40.7 us; the launch traced here: 40.5 us
  Pallas kernels  39.9 us (98%)
  between operations  0.64 us (2%)
    pallas_call x1, Pallas kernels, main(): pl.pallas_call(functools.partial(main_kernel, scale), out_shape=[jax.Shap...  38.7 us
    pallas_call x1, Pallas kernels, finish(): pl.pallas_call(functools.partial(finish_kernel, scale), out_shape=[jax.Sh...  1.23 us

profile of v2, /device:TPU:0, one launch (start us, length us, event | category | flops | bytes accessed | tf_op | source)
XLA Modules:
  0.0 40.5 jit_solution(5194753087346045451)
XLA Ops:
  0.6 38.7 %cycle.1 = (f32[512,512]{1,0:T(8,128)S(1)}, bf16[512,256]{1,0:T(8,128)(2,1)S(1)}, bf16[2,2,256,512]{3,2,1,0:T(8,128)(2,1)S(1)}, f32[2,512]{1,0:T(2,128)S(1)}) custom-call(bf16[512,512]{1,0:T(8,128)(2,1)} %facet_hbm.1, s32[2]{0:T(128)} %ro_hbm.1, s32[2]{0:T(128)} %co_hbm.1, s32[1,512]{1,0:T(1,128)} %bitcast.3, s32[1,512]{1,0:T(1,128)} %bitcast.4, ...), custom_call_target="tpu_custom_call" | custom-call | tf_op jit(solution)/shard_map/cycle/pallas_call | solution.py:510
  39.3 1.2 %finish.1 = (f32[512,512]{1,0:T(8,128)}, f32[2,512]{1,0:T(2,128)}) custom-call(f32[512,512]{1,0:T(8,128)S(1)} %get-tuple-element.6.acc_ref, bf16[512,256]{1,0:T(8,128)(2,1)S(1)} %get-tuple-element.7.last_ref, bf16[2,2,256,512]{3,2,1,0:T(8,128)(2,1)S(1)} %get-tuple-element.8.bt_ref, f32[2,512]{1,0:T(2,128)S(1)} %get-tuple-element.9.res_ref), custom_call_target="tpu_custom_call" | custom-call | tf_op jit(solution)/shard_map/finish/pallas_call | solution.py:587

commit v3 on v2

v3 whole, which is shorter than its diff:
```python
import functools
import math

import jax
import jax.numpy as jnp
from jax import lax
from jax.experimental import pallas as pl
from jax.experimental.pallas import tpu as pltpu
from jax.sharding import PartitionSpec as P

SKY = 65536
SG = 256
NR = 2
NC = 2
f32 = jnp.float32
bf16 = jnp.bfloat16
i32 = jnp.int32
MESH = pl.DeviceIdType.MESH
VM = pl.BlockSpec(memory_space=pltpu.VMEM)
HB = pl.BlockSpec(memory_space=pltpu.HBM)
LIMIT = 32 << 20
ORDER = (
    "p:0", "p:1", "v", "p:2", "p:3",
    "bt", "g:2", "r:0", "r:1", "r:2", "r:3",
    "g:6", "t:0", "t:1", "t:2", "t:3",
    "d:6", "b:0", "b:1", "b:2", "b:3",
    "d:2", "ans", "f:0", "f:1", "own0",
    "f:2", "f:3", "own1", "c:0", "c:1",
    "oth0", "res", "c:2", "c:3",
)

scope = jax.named_scope


def geometry():
    rows = lax.axis_size("frow")
    cols = lax.axis_size("fcol")
    nx = rows // 2
    ny = 1 << ((cols.bit_length() - 1) // 2)
    nz = cols // ny
    return rows, cols, nx, ny, nz


def position():
    _, _, _, ny, _ = geometry()
    frow = lax.axis_index("frow")
    fcol = lax.axis_index("fcol")
    return frow // 2, frow % 2, fcol % ny, fcol // ny


def phase(product):
    k = product & (SKY - 1)
    quarter = lax.shift_right_logical(k + SKY // 8, SKY.bit_length() - 3)
    t = (k - quarter * (SKY // 4)).astype(f32) * (2.0 * math.pi / SKY)
    t2 = t * t
    cos = 1.0 + t2 * (-1 / 2 + t2 * (1 / 24 + t2 * (-1 / 720 + t2 * (1 / 40320))))
    sin = t * (1.0 + t2 * (-1 / 6 + t2 * (1 / 120 + t2 * (-1 / 5040 + t2 * (1 / 362880)))))
    odd = (quarter & 1) == 1
    c = jnp.where(odd, sin, cos)
    s = jnp.where(odd, cos, sin)
    return jnp.where(((quarter + 1) & 2) == 0, c, -c), jnp.where((quarter & 2) == 0, s, -s)


def expand(first, places, c_ref, s_ref):
    n = places.shape[1]
    steps = lax.broadcasted_iota(i32, (16, n), 0)
    c0, s0 = phase(steps * places)
    c1, s1 = phase((first + 16 * steps) * places)
    for k in range(SG // 16):
        ck = c1[k : k + 1]
        sk = s1[k : k + 1]
        c_ref[k * 16 : k * 16 + 16, :] = (ck * c0 - sk * s0).astype(bf16)
        s_ref[k * 16 : k * 16 + 16, :] = (sk * c0 + ck * s0).astype(bf16)


def place(q):
    _, _, _, ny, nz = geometry()
    return lax.div(q, ny * nz), lax.rem(lax.div(q, nz), ny), lax.rem(q, nz)


def device(q, h):
    _, _, _, ny, _ = geometry()
    x, y, z = place(q)
    return (2 * x + h, z * ny + y)


def hots(vis, owned, lanes):
    v = jnp.broadcast_to(vis[1:2].astype(bf16), lanes.shape)
    return owned == vis[0:1], jnp.where(lanes == v, jnp.ones_like(v), jnp.zeros_like(v))


def semaphores():
    plan = {}
    total = 0
    for at, kind in enumerate((
        "plane", "z", "back_z", "back_plane", "cross",
        "facet", "cells", "cells_z", "pair", "pair_z", "values", "answers",
    )):
        count = 4 if at < 5 else 1
        plan[kind] = (at, total, count)
        total += count
    return plan, total


def spread_rows(g_ref, a_tab, c, q, cut):
    wide = g_ref.shape[-1]
    tall = a_tab.shape[1] * a_tab.shape[2]
    first = (((0,), (0,)), ((), ()))
    g = [
        jnp.concatenate([g_ref[c, 2 * q + e, :, :, p].reshape(tall // 2, wide) for e in range(2)], 0)
        for p in range(2)
    ]
    g = jnp.concatenate(g, 1)
    one, two = (
        lax.dot_general(a_tab[p, :, :, cut].reshape(tall, cut.size), g, first, preferred_element_type=f32)
        for p in range(2)
    )
    return jnp.concatenate([one[:, :wide] + two[:, wide:], one[:, wide:] - two[:, :wide]], 1).astype(bf16)


def main_kernel(
    scale, facet_hbm, ro_hbm, co_hbm, sub_hbm, u_hbm, v_hbm, obs_hbm,
    acc_ref, g_ref, a_tab, bt_ref, res_ref,
    facet_ref, ro_ref, co_ref, sub_ref, u_ref, v_ref, obs_ref,
    kl, rc, rs, keep_col, keep_row, p_ref, vis_all, other, z_ref, zb_ref, grid_acc, lanes,
    got, own_z, send_z, got_z, gz, model, vals, pair_vals, slots,
    ssem, rsem, lsem,
):
    rows, cols, nx, ny, nz = geometry()
    x, h, y, z = position()
    chips = nx * ny * nz
    me = (x * ny + y) * nz + z
    fs = facet_ref.shape[0]
    nv = obs_ref.shape[1]
    rows_own = NR * SG // chips
    hr = rows_own // 2
    hlong = nz * hr
    part = 2 * hlong
    wide = SG // 2
    waves = range(4)
    sib = (2 * x + 1 - h, lax.axis_index("fcol"))
    barrier = pltpu.get_barrier_semaphore()

    plane = [(dx, dy) for dx in range(nx) for dy in range(ny)][1:]

    def across(k):
        px, py = lax.rem(x + plane[k][0], nx), lax.rem(y + plane[k][1], ny)
        return px, py, (2 * px + h, z * ny + py)

    def to_z(d):
        return 2 * x + h, lax.rem(z + d, nz) * ny + y

    own_xy = x * ny + y
    near = [sib] + [across(k)[2] for k in range(nx * ny - 1)]
    near += [to_z(d) for d in range(1, nz)]
    for to in near:
        pl.semaphore_signal(barrier, inc=1, device_id=to, device_id_type=MESH)

    def peers(act):
        if chips > 16:
            def step(d, carry):
                to = lax.rem(me + d, chips)
                px, py, pz = place(to)
                act(pz, px * ny + py, to, (2 * px + h, pz * ny + py))
                return carry

            lax.fori_loop(1, chips, step, 0)
            return
        for dx in range(nx):
            for dy in range(ny):
                for dz in range(nz):
                    if dx + dy + dz > 0:
                        px = lax.rem(x + dx, nx)
                        py = lax.rem(y + dy, ny)
                        pz = lax.rem(z + dz, nz)
                        act(pz, px * ny + py, (px * ny + py) * nz + pz, (2 * px + h, pz * ny + py))

    loads = []
    for k, (src, dst) in enumerate((
        (ro_hbm, ro_ref), (co_hbm, co_ref), (sub_hbm, sub_ref), (u_hbm, u_ref), (v_hbm, v_ref),
        (obs_hbm, obs_ref), (facet_hbm, facet_ref),
    )):
        loads.append(pltpu.make_async_copy(src, dst, lsem.at[k]))
        loads[-1].start()
    plan = semaphores()[0]

    def send(kind, w, src, dst, to):
        at, base, _ = plan[kind]
        pltpu.make_async_remote_copy(
            src, dst, ssem.at[at], rsem.at[base + w], device_id=to, device_id_type=MESH
        ).start()

    def land(kind, w, like):
        at, base, _ = plan[kind]
        pltpu.make_async_remote_copy(
            like, like, ssem.at[at], rsem.at[base + w], device_id=sib, device_id_type=MESH
        ).wait_recv()

    def sentall(kind, like):
        at, base, _ = plan[kind]
        pltpu.make_async_remote_copy(
            like, like, ssem.at[at], rsem.at[base], device_id=sib, device_id_type=MESH
        ).wait_send()

    with scope("expandK"):
        expand(0, lax.broadcasted_iota(i32, (1, SG), 1) * (SKY // SG), kl.at[0, :SG], kl.at[0, SG:])
        kl[1, :SG] = kl[0, SG:]
        kl[1, SG:] = -kl[0, :SG]

    def compose(n, places, keep):
        expand(0, places, rc.at[:, :n], rs.at[:, :n])
        for cut in (slice(0, n // 2), slice(n // 2, n)):
            both = jnp.dot(kl[0], rc[:, cut], preferred_element_type=f32)
            both += jnp.dot(kl[1], rs[:, cut], preferred_element_type=f32)
            keep[:, cut] = both

    def shifted(re, im, places, offset):
        cos, sin = phase(offset * places)
        return (re * cos + im * sin).astype(bf16), (im * cos - re * sin).astype(bf16)

    col_places = (lax.axis_index("fcol") * fs + lax.broadcasted_iota(i32, (1, fs), 1)) * (SKY // (cols * fs))
    row_places = (x * (2 * fs) + lax.broadcasted_iota(i32, (1, 2 * fs), 1)) * (SKY // (rows * fs))

    def columns(c):
        re, im = shifted(keep_col[:SG], keep_col[SG:], col_places, co_ref[c])
        for q in range(2):
            bt_ref[c, q, :wide] = re[q * wide : (q + 1) * wide]
            bt_ref[c, q, wide:] = im[q * wide : (q + 1) * wide]

    with scope("composeB"):
        compose(fs, col_places, keep_col)
        loads[0].wait()
        loads[1].wait()
        columns(h)
    with scope("cells"):
        for copy in loads[2:6]:
            copy.wait()
        sub = sub_ref[...]
        row = (lax.rem(sub, NC) * NR + lax.div(sub, NC)) * SG + u_ref[...]
        vis_all[h, z, own_xy, 0:1] = row.astype(f32)
        vis_all[h, z, own_xy, 1:2] = v_ref[...].astype(f32)
        vis_all[h, z, own_xy, 2:4] = obs_ref[...]
    with scope("barwait"):
        pl.semaphore_wait(barrier, len(near))
    for k in range(nx * ny - 1):
        mine = vis_all.at[h, z, own_xy]
        send("cells", 0, mine, mine, across(k)[2])
    send("facet", 0, facet_hbm, other, sib)
    with scope("composeA"):
        compose(2 * fs, row_places, keep_row)
        for r in range(NR):
            pair = shifted(keep_row[:SG], keep_row[SG:], row_places, ro_ref[r])
            for b in range(SG // part):
                blk = r * (SG // part) + b
                for e in range(2):
                    for p in range(2):
                        cut = slice(b * part + e * hlong, b * part + (e + 1) * hlong)
                        a_tab[p, e, blk * hlong : (blk + 1) * hlong] = pair[p][cut]
    loads[6].wait()

    def project(ref, q, base):
        step = fs // 2
        for k in range(2):
            got = lax.dot_general(
                ref[k * step : (k + 1) * step], bt_ref[h, q], (((1,), (1,)), ((), ())),
                preferred_element_type=f32,
            )
            p_ref[pl.ds(pl.multiple_of(base + k * step, step), step)] = got.astype(bf16)

    own_cut = pl.ds(pl.multiple_of(h * fs, fs), fs)

    def produce(w):
        q, e = w // 2, w % 2
        if e == 0:
            project(facet_ref, q, h * fs)
            if q == 0:
                land("facet", 0, other)
            project(other, q, (1 - h) * fs)
        one = jnp.dot(a_tab[0, e], p_ref[...], preferred_element_type=f32)
        two = jnp.dot(a_tab[1, e], p_ref[...], preferred_element_type=f32)
        zr = (one[:, :wide] - two[:, wide:]).reshape(nx, ny, hlong, wide)
        zi = (one[:, wide:] + two[:, :wide]).reshape(nx, ny, hlong, wide)
        z_ref[w, :, :, 0] = zr
        z_ref[w, :, :, 1] = zi
        zb_ref[w, :, :, 0] = zr.astype(bf16)
        zb_ref[w, :, :, 1] = zi.astype(bf16)
        for k in range(nx * ny - 1):
            px, py, to = across(k)
            send("plane", w, zb_ref.at[w, px, py], got.at[w, k], to)

    owned_row = lax.broadcasted_iota(i32, (rows_own, nv), 0)
    owned_row = (x * ny + y) * part + z * hr + (owned_row // hr) * hlong + owned_row % hr
    owned_row = (owned_row + h * (NR * SG)).astype(f32)
    lanes[...] = lax.broadcasted_iota(i32, (SG, nv), 0).astype(f32).astype(bf16)

    def gridding(side, level):
        def one(k):
            vis = vis_all[side, level, k]
            hot_row, hot_col = hots(vis, owned_row, lanes[...])
            parts = [vis[2:3], vis[3:4], jnp.ones_like(vis[0:1])]
            left = jnp.concatenate([jnp.where(hot_row, t, 0.0) for t in parts], 0).astype(bf16)
            return lax.dot_general(left, hot_col, (((1,), (1,)), ((), ())), preferred_element_type=f32)

        def body(t, carry):
            grid_acc[0] += one(2 * t)
            grid_acc[1] += one(2 * t + 1)
            return carry

        lax.fori_loop(0, nx * ny // 2, body, 0)

    def reduce(w):
        land("plane", w, got.at[w])
        total = z_ref[w, x, y]
        for k in range(nx * ny - 1):
            total = total + got[w, k].astype(f32)
        for k in range(nz):
            for p in range(2):
                rows_k = total[p, k * hr : (k + 1) * hr]
                own_z[w, k, :, p * wide : (p + 1) * wide] = rows_k
                send_z[w, k, :, p * wide : (p + 1) * wide] = rows_k.astype(bf16)
        for d in range(1, nz):
            send("z", w, send_z.at[w, lax.rem(z + d, nz)], got_z.at[w, d - 1], to_z(d))

    def turn(w):
        q, e = w // 2, w % 2
        land("z", w, got_z.at[w])
        total = own_z[w, z]
        for d in range(nz - 1):
            total = total + got_z[w, d].astype(f32)
        m = total * scale
        cut = slice(q * wide, (q + 1) * wide)
        rows_of = [slice(p * rows_own + e * hr, p * rows_own + (e + 1) * hr) for p in range(3)]
        sums = [grid_acc[0, k, cut] + grid_acc[1, k, cut] for k in rows_of]
        hat_re = sums[0] - sums[2] * m[:, :wide]
        hat_im = sums[1] - sums[2] * m[:, wide:]
        gz[w, z, :, :wide] = hat_re.astype(bf16)
        gz[w, z, :, wide:] = hat_im.astype(bf16)
        for d in range(1, nz):
            send("back_z", w, gz.at[w, z], gz.at[w, z], to_z(d))
        model[e * hr : (e + 1) * hr, cut] = m[:, :wide]
        model[rows_own + e * hr : rows_own + (e + 1) * hr, cut] = m[:, wide:]

    def over(w, px, py):
        src = g_ref.at[h, w, px, py]
        send("cross", w, src, src, sib)

    def gather(w):
        land("back_z", w, gz.at[w, : nz - 1])
        for k in range(nz):
            cut = slice(k * hr, (k + 1) * hr)
            g_ref[h, w, x, y, 0, cut, :] = gz[w, k, :, :wide]
            g_ref[h, w, x, y, 1, cut, :] = gz[w, k, :, wide:]
        blk = g_ref.at[h, w, x, y]
        for k in range(nx * ny - 1):
            send("back_plane", w, blk, blk, across(k)[2])
        over(w, x, y)

    def finish(w):
        land("back_plane", w, got.at[w])
        for k in range(nx * ny - 1):
            px, py, _ = across(k)
            over(w, px, py)

    def crossed(w):
        land("cross", w, g_ref.at[1 - h, w])

    def degrid(side, level):
        m = model[...].astype(bf16)

        def one(k):
            hot_row, hot_col = hots(vis_all[side, level, k], owned_row, lanes[...])
            val = jnp.dot(m, hot_col, preferred_element_type=f32)
            vr_ = jnp.sum(jnp.where(hot_row, val[:rows_own], 0.0), 0, keepdims=True)
            vi_ = jnp.sum(jnp.where(hot_row, val[rows_own:], 0.0), 0, keepdims=True)
            return jnp.concatenate([vr_, vi_], 0)

        def body(t, carry):
            a = one(2 * t)
            b = one(2 * t + 1)
            vals[side, level, 2 * t] = a
            vals[side, level, 2 * t + 1] = b
            return carry

        lax.fori_loop(0, nx * ny // 2, body, 0)

    def spread(c, q):
        return spread_rows(g_ref, a_tab, c, q, own_cut)

    def image(c, q):
        return jnp.dot(spread(c, q), bt_ref[c, q], preferred_element_type=f32)

    grid_acc[...] = jnp.zeros_like(grid_acc)
    units = 2 * nz
    done = {"grid": 0, "degrid": 0}

    def grid(n):
        for _ in range(n * units // 8):
            k = done["grid"]
            done["grid"] += 1
            side, level = (k, 0) if k < 2 else ((k - 2) // (nz - 1), (k - 2) % (nz - 1) + 1)
            if k == 1:
                land("pair", 0, vis_all.at[1 - h, z])
            if k == 2:
                land("cells_z", 0, vis_all.at[h, : nz - 1])
                for d in range(1, nz):
                    sheet = vis_all.at[h, lax.rem(z + d, nz)]
                    send("pair_z", 0, sheet, sheet, sib)
            if k == nz + 1:
                land("pair_z", 0, vis_all.at[1 - h, : nz - 1])
            with scope("grid%d" % k):
                gridding(h if side == 0 else 1 - h, lax.rem(z + level, nz))

    def ungrid(n):
        for _ in range(n * units // 8):
            k = done["degrid"]
            done["degrid"] += 1
            with scope("degrid%d" % k):
                degrid(1 - h if k < nz else h, lax.rem(z + k % nz, nz))
            if k == nz - 1:
                send("values", 0, vals.at[1 - h], pair_vals, sib)

    def cells():
        land("cells", 0, vis_all.at[h, z, : nx * ny - 1])
        sheet = vis_all.at[h, z]
        for d in range(1, nz):
            send("cells_z", 0, sheet, sheet, to_z(d))
        send("pair", 0, sheet, sheet, sib)

    def answers():
        land("values", 0, pair_vals)
        vals[h] = vals[h] + pair_vals[...]
        peers(lambda pz, pxy, slot, to: send("answers", 0, vals.at[h, pz, pxy], slots.at[me], to))

    def result():
        land("answers", 0, slots.at[: chips - 1])
        start = vals[h, z, own_xy]
        if chips > 16:
            total = lax.fori_loop(1, chips, lambda d, t: t + slots[lax.rem(me + d, chips)], start)
        else:
            total = start
            for d in range(1, chips):
                total = total + slots[lax.rem(me + d, chips)]
        res_ref[...] = obs_ref[...] - total

    def own0():
        acc_ref[...] = image(h, 0)

    def own1():
        acc_ref[...] += image(h, 1)

    def other0():
        acc_ref[...] += image(1 - h, 0)

    acts = {
        "p": produce, "r": reduce, "t": turn, "b": gather, "f": finish, "c": crossed,
    }
    simple = {
        "v": cells, "ans": answers, "res": result, "own0": own0, "own1": own1,
        "oth0": other0, "bt": lambda: columns(1 - h),
    }
    for word in ORDER:
        name, _, arg = word.partition(":")
        if name == "g":
            grid(int(arg))
        elif name == "d":
            ungrid(int(arg))
        else:
            with scope(name + arg):
                acts[name](int(arg)) if arg else simple[name]()
    with scope("drain"):
        for kind, like in (
            ("plane", got), ("z", got_z), ("back_z", got_z), ("back_plane", got),
            ("cross", g_ref.at[h]), ("facet", other), ("cells", vis_all.at[h, z, : nx * ny - 1]),
            ("cells_z", vis_all.at[h, : nz - 1]), ("pair", vis_all.at[h, z]),
            ("pair_z", vis_all.at[h, : nz - 1]), ("values", pair_vals), ("answers", slots.at[: chips - 1]),
        ):
            sentall(kind, like)


def main(ro, co, sub, u, v, obs, facet, scale):
    _, _, nx, ny, nz = geometry()
    chips = nx * ny * nz
    fs = facet.shape[0]
    nv = obs.shape[1]
    rows_own = NR * SG // chips
    hr = rows_own // 2
    hlong = nz * hr
    wide = SG // 2
    plan, total = semaphores()
    dma = pltpu.SemaphoreType.DMA
    return pl.pallas_call(
        functools.partial(main_kernel, scale),
        out_shape=[
            jax.ShapeDtypeStruct((fs, fs), f32),
            jax.ShapeDtypeStruct((2, 4, nx, ny, 2, hlong, wide), bf16),
            jax.ShapeDtypeStruct((2, 2, nx * ny * hlong, 2 * fs), bf16),
            jax.ShapeDtypeStruct((NC, 2, SG, fs), bf16),
            jax.ShapeDtypeStruct((2, nv), f32),
        ],
        in_specs=[HB] * 7,
        out_specs=[VM] * 5,
        scratch_shapes=[
            pltpu.VMEM((fs, fs), bf16),
            pltpu.SMEM((NR,), i32),
            pltpu.SMEM((NC,), i32),
            pltpu.VMEM((1, nv), i32),
            pltpu.VMEM((1, nv), i32),
            pltpu.VMEM((1, nv), i32),
            pltpu.VMEM((2, nv), f32),
            pltpu.VMEM((2, 2 * SG, SG), bf16),
            pltpu.VMEM((SG, 2 * fs), bf16),
            pltpu.VMEM((SG, 2 * fs), bf16),
            pltpu.VMEM((2 * SG, fs), f32),
            pltpu.VMEM((2 * SG, 2 * fs), f32),
            pltpu.VMEM((2 * fs, SG), bf16),
            pltpu.VMEM((2, nz, nx * ny, 4, nv), f32),
            pltpu.VMEM((fs, fs), bf16),
            pltpu.VMEM((4, nx, ny, 2, hlong, wide), f32),
            pltpu.VMEM((4, nx, ny, 2, hlong, wide), bf16),
            pltpu.VMEM((2, 3 * rows_own, SG), f32),
            pltpu.VMEM((SG, nv), bf16),
            pltpu.VMEM((4, nx * ny - 1, 2, hlong, wide), bf16),
            pltpu.VMEM((4, nz, hr, SG), f32),
            pltpu.VMEM((4, nz, hr, SG), bf16),
            pltpu.VMEM((4, nz - 1, hr, SG), bf16),
            pltpu.VMEM((4, nz, hr, SG), bf16),
            pltpu.VMEM((2 * rows_own, SG), f32),
            pltpu.VMEM((2, nz, nx * ny, 2, nv), f32),
            pltpu.VMEM((nz, nx * ny, 2, nv), f32),
            pltpu.VMEM((chips, 2, nv), f32),
            dma((len(plan),)),
            dma((total,)),
            dma((8,)),
        ],
        compiler_params=pltpu.CompilerParams(
            collective_id=0, has_side_effects=True, vmem_limit_bytes=LIMIT
        ),
        name="cycle",
    )(*(pltpu.with_memory_space_constraint(a, pltpu.HBM) for a in (facet, ro, co, sub, u, v, obs)))


def finish_kernel(scale, acc_ref, g_ref, a_tab, bt_ref, res_ref, image_hbm, out_hbm, buf, sem):
    _, h, _, _ = position()
    fs = acc_ref.shape[0]
    pieces = sem.shape[0] - 1
    step = fs // pieces
    copies = [pltpu.make_async_copy(res_ref, out_hbm, sem.at[pieces])]
    copies[0].start()
    for k in range(pieces):
        cut = slice(k * step, (k + 1) * step)
        u = spread_rows(g_ref, a_tab, 1 - h, 1, pl.ds(pl.multiple_of(h * fs + k * step, step), step))
        buf[cut] = (acc_ref[cut] + jnp.dot(u, bt_ref[1 - h, 1], preferred_element_type=f32)) * scale
        copies.append(pltpu.make_async_copy(buf.at[cut], image_hbm.at[cut], sem.at[k]))
        copies[-1].start()
    for copy in copies:
        copy.wait()


def finish(acc, g, a_tab, bt, res, scale):
    fs = acc.shape[0]
    return pl.pallas_call(
        functools.partial(finish_kernel, scale),
        out_shape=[jax.ShapeDtypeStruct((fs, fs), f32), jax.ShapeDtypeStruct(res.shape, f32)],
        in_specs=[VM] * 5,
        out_specs=[HB] * 2,
        scratch_shapes=[pltpu.VMEM((fs, fs), f32), pltpu.SemaphoreType.DMA((3,))],
        compiler_params=pltpu.CompilerParams(vmem_limit_bytes=6 << 20),
        name="finish",
    )(acc, g, a_tab, bt, res)


def shards(facet_image, row_offsets, col_offsets, vis_subgrid, vis_u, vis_v, observed):
    rows, cols, _, _, _ = geometry()
    fs = facet_image.shape[0]
    scale_in = 1.0 / (fs * math.sqrt(rows * cols))
    scale_out = 1.0 / (SG * math.sqrt(NR * NC))
    acc, g, a_tab, bt, residual = main(
        row_offsets, col_offsets, vis_subgrid[None], vis_u[None], vis_v[None],
        observed, facet_image, scale_in / SG,
    )
    return tuple(finish(acc, g, a_tab, bt, residual, scale_out / SG))


def solution(mesh):
    in_specs = (
        P("frow", "fcol"),
        P(),
        P(),
        P(("frow", "fcol")),
        P(("frow", "fcol")),
        P(("frow", "fcol")),
        P(None, ("frow", "fcol")),
    )
    out_specs = (P("frow", "fcol"), P(None, ("frow", "fcol")))
    return jax.shard_map(shards, mesh=mesh, in_specs=in_specs, out_specs=out_specs, check_vma=False)
```

time: 40.7 us -> 36 us (0.88)
  Pallas kernels: 39.9 us -> 35.2 us
    pallas_call x1, Pallas kernels: 38.7 us -> 33.6 us  [main(): pl.pallas_call(functools.partial(main_kernel, scale), out_shape=[jax.Shap...]
where the time goes in v3:
time: 36 us; the launch traced here: 35.8 us
  Pallas kernels  35.2 us (98%)
  between operations  0.64 us (2%)
    pallas_call x1, Pallas kernels, main(): pl.pallas_call(functools.partial(main_kernel, scale), out_shape=[jax.Shap...  33.6 us
    pallas_call x1, Pallas kernels, finish(): pl.pallas_call(functools.partial(finish_kernel, scale), out_shape=[jax.Sh...  1.61 us

profile of v3, /device:TPU:0, one launch (start us, length us, event | category | flops | bytes accessed | tf_op | source)
XLA Modules:
  0.0 35.8 jit_solution(10367737328610246874)
XLA Ops:
  0.6 33.6 %cycle.1 = (f32[512,512]{1,0:T(8,128)S(1)}, bf16[2,4,2,2,2,64,128]{6,5,4,3,2,1,0:T(8,128)(2,1)S(1)}, bf16[2,2,256,1024]{3,2,1,0:T(8,128)(2,1)S(1)}, bf16[2,2,256,512]{3,2,1,0:T(8,128)(2,1)S(1)}, f32[2,512]{1,0:T(2,128)S(1)}) custom-call(bf16[512,512]{1,0:T(8,128)(2,1)} %facet_hbm.1, s32[2]{0:T(128)} %ro_hbm.1, s32[2]{0:T(128)} %co_hbm.1, s32[1,512]{1,0:T(1,128)} %bitcast.3, ...), custom_call_target="tpu_custom_call" | custom-call | tf_op jit(solution)/shard_map/cycle/pallas_call | solution.py:491
  34.2 1.6 %finish.1 = (f32[512,512]{1,0:T(8,128)}, f32[2,512]{1,0:T(2,128)}) custom-call(f32[512,512]{1,0:T(8,128)S(1)} %get-tuple-element.7.acc_ref, bf16[2,4,2,2,2,64,128]{6,5,4,3,2,1,0:T(8,128)(2,1)S(1)} %get-tuple-element.8.g_ref, bf16[2,2,256,1024]{3,2,1,0:T(8,128)(2,1)S(1)} %get-tuple-element.9.a_tab, bf16[2,2,256,512]{3,2,1,0:T(8,128)(2,1)S(1)} %get-tuple-element.10.bt_ref, ...), custom_call_target="tpu_custom_call" | custom-call | tf_op jit(solution)/shard_map/finish/pallas_call | solution.py:561

commit v4 on v3

--- a/solution.py
+++ b/solution.py
@@ -20,13 +20,15 @@
 HB = pl.BlockSpec(memory_space=pltpu.HBM)
 LIMIT = 32 << 20
 ORDER = (
-    "p:0", "p:1", "v", "p:2", "p:3",
-    "bt", "g:2", "r:0", "r:1", "r:2", "r:3",
-    "g:6", "t:0", "t:1", "t:2", "t:3",
-    "d:6", "b:0", "b:1", "b:2", "b:3",
-    "d:2", "ans", "f:0", "f:1", "own0",
-    "f:2", "f:3", "own1", "c:0", "c:1",
-    "oth0", "res", "c:2", "c:3",
+    "p:0", "rows1", "p:1", "v", "cols1",
+    "p:2", "p:3", "bt", "g:1", "r:0",
+    "r:1", "g:1", "r:2", "g:2", "x", "r:3",
+    "t:0", "t:1", "t:2", "t:3", "m",
+    "b:0", "d:1", "b:1", "d:1", "b:2", "d:2",
+    "ans", "b:3", "f:0", "own:0", "f:1", "own:1",
+    "c:0", "oth:0", "f:2", "own:2", "c:1", "oth:1",
+    "res", "f:3", "c:2", "oth:2",
+    "own:3", "c:3",
 )
 
 scope = jax.named_scope
@@ -85,8 +87,25 @@
 
 
 def hots(vis, owned, lanes):
-    v = jnp.broadcast_to(vis[1:2].astype(bf16), lanes.shape)
-    return owned == vis[0:1], jnp.where(lanes == v, jnp.ones_like(v), jnp.zeros_like(v))
+    n = lanes.shape[1]
+    parts = []
+    for t in range(0, vis.shape[1], n):
+        v = jnp.broadcast_to(vis[1:2, t : t + n].astype(bf16), lanes.shape)
+        parts.append(jnp.where(lanes == v, jnp.ones_like(v), jnp.zeros_like(v)))
+    return owned == vis[0:1], jnp.concatenate(parts, 1)
+
+
+def pairs(count, body):
+    if count <= 4:
+        for t in range(0, count, 2):
+            body(t)
+        return
+
+    def step(t, carry):
+        body(2 * t)
+        return carry
+
+    lax.fori_loop(0, count // 2, step, 0)
 
 
 def semaphores():
@@ -94,7 +113,7 @@
     total = 0
     for at, kind in enumerate((
         "plane", "z", "back_z", "back_plane", "cross",
-        "facet", "cells", "cells_z", "pair", "pair_z", "values", "answers",
+        "facet", "cells", "cells_z", "sums", "model", "answers",
     )):
         count = 4 if at < 5 else 1
         plan[kind] = (at, total, count)
@@ -102,28 +121,24 @@
     return plan, total
 
 
-def spread_rows(g_ref, a_tab, c, q, cut):
+def spread_rows(g_ref, a_tab, c, w, cut):
     wide = g_ref.shape[-1]
-    tall = a_tab.shape[1] * a_tab.shape[2]
+    tall = a_tab.shape[2]
+    e = w % 2
     first = (((0,), (0,)), ((), ()))
-    g = [
-        jnp.concatenate([g_ref[c, 2 * q + e, :, :, p].reshape(tall // 2, wide) for e in range(2)], 0)
-        for p in range(2)
-    ]
-    g = jnp.concatenate(g, 1)
+    g = jnp.concatenate([g_ref[c, w, :, :, p].reshape(tall, wide) for p in range(2)], 1)
     one, two = (
-        lax.dot_general(a_tab[p, :, :, cut].reshape(tall, cut.size), g, first, preferred_element_type=f32)
-        for p in range(2)
+        lax.dot_general(a_tab[p, e, :, cut], g, first, preferred_element_type=f32) for p in range(2)
     )
-    return jnp.concatenate([one[:, :wide] + two[:, wide:], one[:, wide:] - two[:, :wide]], 1).astype(bf16)
+    return jnp.concatenate([one[:, :wide] + two[:, wide:], one[:, wide:] - two[:, :wide]], 1)
 
 
 def main_kernel(
     scale, facet_hbm, ro_hbm, co_hbm, sub_hbm, u_hbm, v_hbm, obs_hbm,
-    acc_ref, g_ref, a_tab, bt_ref, res_ref,
+    acc_ref, g_ref, a_tab, bt_ref, res_ref, half_u,
     facet_ref, ro_ref, co_ref, sub_ref, u_ref, v_ref, obs_ref,
-    kl, rc, rs, keep_col, keep_row, p_ref, vis_all, other, z_ref, zb_ref, grid_acc, lanes,
-    got, own_z, send_z, got_z, gz, model, vals, pair_vals, slots,
+    kk, ks, kcol, krow, cc, cs, rc, rs, keep_col, keep_row, p_ref, vis_all, other, z_ref, zb_ref, grid_acc, own_sum, pair_sum, got_sum, own_model, got_model, lanes,
+    got, own_z, send_z, got_z, gz, model, vals, slots,
     ssem, rsem, lsem,
 ):
     rows, cols, nx, ny, nz = geometry()
@@ -203,59 +218,73 @@
         ).wait_send()
 
     with scope("expandK"):
-        expand(0, lax.broadcasted_iota(i32, (1, SG), 1) * (SKY // SG), kl.at[0, :SG], kl.at[0, SG:])
-        kl[1, :SG] = kl[0, SG:]
-        kl[1, SG:] = -kl[0, :SG]
-
-    def compose(n, places, keep):
-        expand(0, places, rc.at[:, :n], rs.at[:, :n])
-        for cut in (slice(0, n // 2), slice(n // 2, n)):
-            both = jnp.dot(kl[0], rc[:, cut], preferred_element_type=f32)
-            both += jnp.dot(kl[1], rs[:, cut], preferred_element_type=f32)
-            keep[:, cut] = both
-
-    def shifted(re, im, places, offset):
-        cos, sin = phase(offset * places)
-        return (re * cos + im * sin).astype(bf16), (im * cos - re * sin).astype(bf16)
-
+        expand(0, lax.broadcasted_iota(i32, (1, SG), 1) * (SKY // SG), kk, ks)
+        for q in range(2):
+            cut = slice(q * wide, (q + 1) * wide)
+            kcol[0, q, :wide] = kk[cut]
+            kcol[0, q, wide:] = ks[cut]
+            kcol[1, q, :wide] = ks[cut]
+            kcol[1, q, wide:] = -kk[cut]
     col_places = (lax.axis_index("fcol") * fs + lax.broadcasted_iota(i32, (1, fs), 1)) * (SKY // (cols * fs))
     row_places = (x * (2 * fs) + lax.broadcasted_iota(i32, (1, 2 * fs), 1)) * (SKY // (rows * fs))
 
-    def columns(c):
-        re, im = shifted(keep_col[:SG], keep_col[SG:], col_places, co_ref[c])
-        for q in range(2):
-            bt_ref[c, q, :wide] = re[q * wide : (q + 1) * wide]
-            bt_ref[c, q, wide:] = im[q * wide : (q + 1) * wide]
-
-    with scope("composeB"):
-        compose(fs, col_places, keep_col)
+    def compose(k0, k1, c_ref, s_ref, out):
+        n = c_ref.shape[1]
+        for cut in (slice(0, n // 2), slice(n // 2, n)):
+            both = jnp.dot(k0, c_ref[:, cut], preferred_element_type=f32)
+            both += jnp.dot(k1, s_ref[:, cut], preferred_element_type=f32)
+            out[:, cut] = both
+
+    def shifted(both, places, offset):
+        cos, sin = phase(offset * places)
+        re = both[:wide]
+        im = both[wide:]
+        return (re * cos + im * sin).astype(bf16), (im * cos - re * sin).astype(bf16)
+
+    def columns(c, q):
+        bt_ref[c, q, :wide], bt_ref[c, q, wide:] = shifted(keep_col[q], col_places, co_ref[c])
+
+    def columns_half(q):
+        compose(kcol[0, q], kcol[1, q], cc, cs, keep_col.at[q])
+        columns(h, q)
+
+    def rows_half(e):
+        compose(krow[0, e], krow[1, e], rc, rs, keep_row)
+        for r in range(NR):
+            cut = slice(r * wide, (r + 1) * wide)
+            a_tab[0, e, cut], a_tab[1, e, cut] = shifted(keep_row[...], row_places, ro_ref[r])
+
+    with scope("columns0"):
+        expand(0, col_places, cc, cs)
         loads[0].wait()
         loads[1].wait()
-        columns(h)
+        columns_half(0)
     with scope("cells"):
         for copy in loads[2:6]:
             copy.wait()
         sub = sub_ref[...]
         row = (lax.rem(sub, NC) * NR + lax.div(sub, NC)) * SG + u_ref[...]
-        vis_all[h, z, own_xy, 0:1] = row.astype(f32)
-        vis_all[h, z, own_xy, 1:2] = v_ref[...].astype(f32)
-        vis_all[h, z, own_xy, 2:4] = obs_ref[...]
+        vis_all[z, own_xy, 0:1] = row.astype(f32)
+        vis_all[z, own_xy, 1:2] = v_ref[...].astype(f32)
+        vis_all[z, own_xy, 2:4] = obs_ref[...]
     with scope("barwait"):
         pl.semaphore_wait(barrier, len(near))
+    send("facet", 0, facet_hbm, other, sib)
     for k in range(nx * ny - 1):
-        mine = vis_all.at[h, z, own_xy]
+        mine = vis_all.at[z, own_xy]
         send("cells", 0, mine, mine, across(k)[2])
-    send("facet", 0, facet_hbm, other, sib)
-    with scope("composeA"):
-        compose(2 * fs, row_places, keep_row)
-        for r in range(NR):
-            pair = shifted(keep_row[:SG], keep_row[SG:], row_places, ro_ref[r])
+    with scope("rows0"):
+        for e in range(2):
             for b in range(SG // part):
-                blk = r * (SG // part) + b
-                for e in range(2):
-                    for p in range(2):
-                        cut = slice(b * part + e * hlong, b * part + (e + 1) * hlong)
-                        a_tab[p, e, blk * hlong : (blk + 1) * hlong] = pair[p][cut]
+                src = slice(b * part + e * hlong, b * part + (e + 1) * hlong)
+                dst = slice(b * hlong, (b + 1) * hlong)
+                low = slice(wide + b * hlong, wide + (b + 1) * hlong)
+                krow[0, e, dst] = kk[src]
+                krow[0, e, low] = ks[src]
+                krow[1, e, dst] = ks[src]
+                krow[1, e, low] = -kk[src]
+        expand(0, row_places, rc, rs)
+        rows_half(0)
     loads[6].wait()
 
     def project(ref, q, base):
@@ -288,25 +317,27 @@
             px, py, to = across(k)
             send("plane", w, zb_ref.at[w, px, py], got.at[w, k], to)
 
-    owned_row = lax.broadcasted_iota(i32, (rows_own, nv), 0)
+    owned_row = lax.broadcasted_iota(i32, (2 * rows_own, nv), 0)
+    column = owned_row // rows_own
+    column = h + column - 2 * h * column
+    owned_row = owned_row % rows_own
     owned_row = (x * ny + y) * part + z * hr + (owned_row // hr) * hlong + owned_row % hr
-    owned_row = (owned_row + h * (NR * SG)).astype(f32)
-    lanes[...] = lax.broadcasted_iota(i32, (SG, nv), 0).astype(f32).astype(bf16)
-
-    def gridding(side, level):
+    owned_row = (owned_row + column * (NR * SG)).astype(f32)
+    lanes[...] = lax.broadcasted_iota(i32, lanes.shape, 0).astype(f32).astype(bf16)
+
+    def gridding(level):
         def one(k):
-            vis = vis_all[side, level, k]
+            vis = vis_all[level, k]
             hot_row, hot_col = hots(vis, owned_row, lanes[...])
             parts = [vis[2:3], vis[3:4], jnp.ones_like(vis[0:1])]
             left = jnp.concatenate([jnp.where(hot_row, t, 0.0) for t in parts], 0).astype(bf16)
             return lax.dot_general(left, hot_col, (((1,), (1,)), ((), ())), preferred_element_type=f32)
 
-        def body(t, carry):
-            grid_acc[0] += one(2 * t)
-            grid_acc[1] += one(2 * t + 1)
-            return carry
-
-        lax.fori_loop(0, nx * ny // 2, body, 0)
+        def body(k):
+            grid_acc[0] += one(k)
+            grid_acc[1] += one(k + 1)
+
+        pairs(nx * ny, body)
 
     def reduce(w):
         land("plane", w, got.at[w])
@@ -323,14 +354,16 @@
 
     def turn(w):
         q, e = w // 2, w % 2
+        if w == 0:
+            land("sums", 0, got_sum)
         land("z", w, got_z.at[w])
         total = own_z[w, z]
         for d in range(nz - 1):
             total = total + got_z[w, d].astype(f32)
         m = total * scale
         cut = slice(q * wide, (q + 1) * wide)
-        rows_of = [slice(p * rows_own + e * hr, p * rows_own + (e + 1) * hr) for p in range(3)]
-        sums = [grid_acc[0, k, cut] + grid_acc[1, k, cut] for k in rows_of]
+        half = slice(e * hr, (e + 1) * hr)
+        sums = [own_sum[p, half, cut] + got_sum[p, half, cut] for p in range(3)]
         hat_re = sums[0] - sums[2] * m[:, :wide]
         hat_im = sums[1] - sums[2] * m[:, wide:]
         gz[w, z, :, :wide] = hat_re.astype(bf16)
@@ -364,76 +397,88 @@
     def crossed(w):
         land("cross", w, g_ref.at[1 - h, w])
 
-    def degrid(side, level):
-        m = model[...].astype(bf16)
+    def degrid(level):
+        m = jnp.concatenate([own_model[...], got_model[...]], 0)
 
         def one(k):
-            hot_row, hot_col = hots(vis_all[side, level, k], owned_row, lanes[...])
+            hot_row, hot_col = hots(vis_all[level, k], owned_row, lanes[...])
             val = jnp.dot(m, hot_col, preferred_element_type=f32)
-            vr_ = jnp.sum(jnp.where(hot_row, val[:rows_own], 0.0), 0, keepdims=True)
-            vi_ = jnp.sum(jnp.where(hot_row, val[rows_own:], 0.0), 0, keepdims=True)
-            return jnp.concatenate([vr_, vi_], 0)
-
-        def body(t, carry):
-            a = one(2 * t)
-            b = one(2 * t + 1)
-            vals[side, level, 2 * t] = a
-            vals[side, level, 2 * t + 1] = b
-            return carry
-
-        lax.fori_loop(0, nx * ny // 2, body, 0)
-
-    def spread(c, q):
-        return spread_rows(g_ref, a_tab, c, q, own_cut)
-
-    def image(c, q):
-        return jnp.dot(spread(c, q), bt_ref[c, q], preferred_element_type=f32)
+            out = []
+            for p in range(2):
+                picked = [
+                    jnp.where(hot_row[c * rows_own : (c + 1) * rows_own], val[(2 * c + p) * rows_own : (2 * c + p + 1) * rows_own], 0.0)
+                    for c in range(2)
+                ]
+                out.append(jnp.sum(picked[0] + picked[1], 0, keepdims=True))
+            return jnp.concatenate(out, 0)
+
+        def body(k):
+            a = one(k)
+            b = one(k + 1)
+            vals[level, k] = a
+            vals[level, k + 1] = b
+
+        pairs(nx * ny, body)
+
+    def image(side, w):
+        c = h if side == 0 else 1 - h
+        q, e = w // 2, w % 2
+        u = spread_rows(g_ref, a_tab, c, w, own_cut)
+        if e == 0:
+            half_u[side] = u
+            return
+        total = (half_u[side] + u).astype(bf16)
+        got = jnp.dot(total, bt_ref[c, q], preferred_element_type=f32)
+        if q == 0 and side == 0:
+            acc_ref[...] = got
+        else:
+            acc_ref[...] += got
 
     grid_acc[...] = jnp.zeros_like(grid_acc)
-    units = 2 * nz
     done = {"grid": 0, "degrid": 0}
 
     def grid(n):
-        for _ in range(n * units // 8):
+        for _ in range(n * nz // 4):
             k = done["grid"]
             done["grid"] += 1
-            side, level = (k, 0) if k < 2 else ((k - 2) // (nz - 1), (k - 2) % (nz - 1) + 1)
             if k == 1:
-                land("pair", 0, vis_all.at[1 - h, z])
-            if k == 2:
-                land("cells_z", 0, vis_all.at[h, : nz - 1])
-                for d in range(1, nz):
-                    sheet = vis_all.at[h, lax.rem(z + d, nz)]
-                    send("pair_z", 0, sheet, sheet, sib)
-            if k == nz + 1:
-                land("pair_z", 0, vis_all.at[1 - h, : nz - 1])
+                land("cells_z", 0, vis_all.at[: nz - 1])
             with scope("grid%d" % k):
-                gridding(h if side == 0 else 1 - h, lax.rem(z + level, nz))
+                gridding(lax.rem(z + k, nz))
+
+    def exchange():
+        for p in range(3):
+            base = 2 * p * rows_own
+            total = grid_acc[0, base : base + 2 * rows_own] + grid_acc[1, base : base + 2 * rows_own]
+            own_sum[p] = total[:rows_own]
+            pair_sum[p] = total[rows_own:]
+        send("sums", 0, pair_sum, got_sum, sib)
+
+    def models():
+        own_model[...] = model[...].astype(bf16)
+        send("model", 0, own_model, got_model, sib)
 
     def ungrid(n):
-        for _ in range(n * units // 8):
+        for _ in range(n * nz // 4):
             k = done["degrid"]
             done["degrid"] += 1
+            if k == 0:
+                land("model", 0, got_model)
             with scope("degrid%d" % k):
-                degrid(1 - h if k < nz else h, lax.rem(z + k % nz, nz))
-            if k == nz - 1:
-                send("values", 0, vals.at[1 - h], pair_vals, sib)
+                degrid(lax.rem(z + k, nz))
 
     def cells():
-        land("cells", 0, vis_all.at[h, z, : nx * ny - 1])
-        sheet = vis_all.at[h, z]
+        land("cells", 0, vis_all.at[z, : nx * ny - 1])
+        sheet = vis_all.at[z]
         for d in range(1, nz):
             send("cells_z", 0, sheet, sheet, to_z(d))
-        send("pair", 0, sheet, sheet, sib)
 
     def answers():
-        land("values", 0, pair_vals)
-        vals[h] = vals[h] + pair_vals[...]
-        peers(lambda pz, pxy, slot, to: send("answers", 0, vals.at[h, pz, pxy], slots.at[me], to))
+        peers(lambda pz, pxy, slot, to: send("answers", 0, vals.at[pz, pxy], slots.at[me], to))
 
     def result():
         land("answers", 0, slots.at[: chips - 1])
-        start = vals[h, z, own_xy]
+        start = vals[z, own_xy]
         if chips > 16:
             total = lax.fori_loop(1, chips, lambda d, t: t + slots[lax.rem(me + d, chips)], start)
         else:
@@ -442,21 +487,17 @@
                 total = total + slots[lax.rem(me + d, chips)]
         res_ref[...] = obs_ref[...] - total
 
-    def own0():
-        acc_ref[...] = image(h, 0)
-
-    def own1():
-        acc_ref[...] += image(h, 1)
-
-    def other0():
-        acc_ref[...] += image(1 - h, 0)
+    def late_columns():
+        columns(1 - h, 0)
+        columns(1 - h, 1)
 
     acts = {
         "p": produce, "r": reduce, "t": turn, "b": gather, "f": finish, "c": crossed,
+        "own": lambda w: image(0, w), "oth": lambda w: image(1, w),
     }
     simple = {
-        "v": cells, "ans": answers, "res": result, "own0": own0, "own1": own1,
-        "oth0": other0, "bt": lambda: columns(1 - h),
+        "v": cells, "ans": answers, "res": result, "x": exchange, "m": models,
+        "rows1": lambda: rows_half(1), "cols1": lambda: columns_half(1), "bt": late_columns,
     }
     for word in ORDER:
         name, _, arg = word.partition(":")
@@ -470,9 +511,8 @@
     with scope("drain"):
         for kind, like in (
             ("plane", got), ("z", got_z), ("back_z", got_z), ("back_plane", got),
-            ("cross", g_ref.at[h]), ("facet", other), ("cells", vis_all.at[h, z, : nx * ny - 1]),
-            ("cells_z", vis_all.at[h, : nz - 1]), ("pair", vis_all.at[h, z]),
-            ("pair_z", vis_all.at[h, : nz - 1]), ("values", pair_vals), ("answers", slots.at[: chips - 1]),
+            ("cross", g_ref.at[h]), ("facet", other), ("cells", vis_all.at[z, : nx * ny - 1]),
+            ("cells_z", vis_all.at[: nz - 1]), ("sums", got_sum), ("model", got_model), ("answers", slots.at[: chips - 1]),
         ):
             sentall(kind, like)
 
@@ -496,9 +536,10 @@
             jax.ShapeDtypeStruct((2, 2, nx * ny * hlong, 2 * fs), bf16),
             jax.ShapeDtypeStruct((NC, 2, SG, fs), bf16),
             jax.ShapeDtypeStruct((2, nv), f32),
+            jax.ShapeDtypeStruct((2, fs, SG), f32),
         ],
         in_specs=[HB] * 7,
-        out_specs=[VM] * 5,
+        out_specs=[VM] * 6,
         scratch_shapes=[
             pltpu.VMEM((fs, fs), bf16),
             pltpu.SMEM((NR,), i32),
@@ -507,25 +548,34 @@
             pltpu.VMEM((1, nv), i32),
             pltpu.VMEM((1, nv), i32),
             pltpu.VMEM((2, nv), f32),
-            pltpu.VMEM((2, 2 * SG, SG), bf16),
+            pltpu.VMEM((SG, SG), bf16),
+            pltpu.VMEM((SG, SG), bf16),
+            pltpu.VMEM((2, 2, SG, SG), bf16),
+            pltpu.VMEM((2, 2, SG, SG), bf16),
+            pltpu.VMEM((SG, fs), bf16),
+            pltpu.VMEM((SG, fs), bf16),
             pltpu.VMEM((SG, 2 * fs), bf16),
             pltpu.VMEM((SG, 2 * fs), bf16),
-            pltpu.VMEM((2 * SG, fs), f32),
-            pltpu.VMEM((2 * SG, 2 * fs), f32),
+            pltpu.VMEM((2, SG, fs), f32),
+            pltpu.VMEM((SG, 2 * fs), f32),
             pltpu.VMEM((2 * fs, SG), bf16),
-            pltpu.VMEM((2, nz, nx * ny, 4, nv), f32),
+            pltpu.VMEM((nz, nx * ny, 4, nv), f32),
             pltpu.VMEM((fs, fs), bf16),
             pltpu.VMEM((4, nx, ny, 2, hlong, wide), f32),
             pltpu.VMEM((4, nx, ny, 2, hlong, wide), bf16),
-            pltpu.VMEM((2, 3 * rows_own, SG), f32),
-            pltpu.VMEM((SG, nv), bf16),
+            pltpu.VMEM((2, 6 * rows_own, SG), f32),
+            pltpu.VMEM((3, rows_own, SG), f32),
+            pltpu.VMEM((3, rows_own, SG), f32),
+            pltpu.VMEM((3, rows_own, SG), f32),
+            pltpu.VMEM((2 * rows_own, SG), bf16),
+            pltpu.VMEM((2 * rows_own, SG), bf16),
+            pltpu.VMEM((SG, 128), bf16),
             pltpu.VMEM((4, nx * ny - 1, 2, hlong, wide), bf16),
             pltpu.VMEM((4, nz, hr, SG), f32),
             pltpu.VMEM((4, nz, hr, SG), bf16),
             pltpu.VMEM((4, nz - 1, hr, SG), bf16),
             pltpu.VMEM((4, nz, hr, SG), bf16),
             pltpu.VMEM((2 * rows_own, SG), f32),
-            pltpu.VMEM((2, nz, nx * ny, 2, nv), f32),
             pltpu.VMEM((nz, nx * ny, 2, nv), f32),
             pltpu.VMEM((chips, 2, nv), f32),
             dma((len(plan),)),
@@ -539,7 +589,7 @@
     )(*(pltpu.with_memory_space_constraint(a, pltpu.HBM) for a in (facet, ro, co, sub, u, v, obs)))
 
 
-def finish_kernel(scale, acc_ref, g_ref, a_tab, bt_ref, res_ref, image_hbm, out_hbm, buf, sem):
+def finish_kernel(scale, acc_ref, g_ref, a_tab, bt_ref, res_ref, half_u, image_hbm, out_hbm, buf, sem):
     _, h, _, _ = position()
     fs = acc_ref.shape[0]
     pieces = sem.shape[0] - 1
@@ -548,7 +598,8 @@
     copies[0].start()
     for k in range(pieces):
         cut = slice(k * step, (k + 1) * step)
-        u = spread_rows(g_ref, a_tab, 1 - h, 1, pl.ds(pl.multiple_of(h * fs + k * step, step), step))
+        u = spread_rows(g_ref, a_tab, 1 - h, 3, pl.ds(pl.multiple_of(h * fs + k * step, step), step))
+        u = (half_u[1, cut] + u).astype(bf16)
         buf[cut] = (acc_ref[cut] + jnp.dot(u, bt_ref[1 - h, 1], preferred_element_type=f32)) * scale
         copies.append(pltpu.make_async_copy(buf.at[cut], image_hbm.at[cut], sem.at[k]))
         copies[-1].start()
@@ -556,17 +607,17 @@
         copy.wait()
 
 
-def finish(acc, g, a_tab, bt, res, scale):
+def finish(acc, g, a_tab, bt, res, u, scale):
     fs = acc.shape[0]
     return pl.pallas_call(
         functools.partial(finish_kernel, scale),
         out_shape=[jax.ShapeDtypeStruct((fs, fs), f32), jax.ShapeDtypeStruct(res.shape, f32)],
-        in_specs=[VM] * 5,
+        in_specs=[VM] * 6,
         out_specs=[HB] * 2,
         scratch_shapes=[pltpu.VMEM((fs, fs), f32), pltpu.SemaphoreType.DMA((3,))],
         compiler_params=pltpu.CompilerParams(vmem_limit_bytes=6 << 20),
         name="finish",
-    )(acc, g, a_tab, bt, res)
+    )(acc, g, a_tab, bt, res, u)
 
 
 def shards(facet_image, row_offsets, col_offsets, vis_subgrid, vis_u, vis_v, observed):
@@ -574,11 +625,11 @@
     fs = facet_image.shape[0]
     scale_in = 1.0 / (fs * math.sqrt(rows * cols))
     scale_out = 1.0 / (SG * math.sqrt(NR * NC))
-    acc, g, a_tab, bt, residual = main(
+    acc, g, a_tab, bt, residual, u = main(
         row_offsets, col_offsets, vis_subgrid[None], vis_u[None], vis_v[None],
         observed, facet_image, scale_in / SG,
     )
-    return tuple(finish(acc, g, a_tab, bt, residual, scale_out / SG))
+    return tuple(finish(acc, g, a_tab, bt, residual, u, scale_out / SG))
 
 
 def solution(mesh):

time: 36 us -> 33.7 us (0.936)
  Pallas kernels: 35.2 us -> 32.9 us
    pallas_call x1, Pallas kernels: 33.6 us -> 31.4 us  [main(): pl.pallas_call(functools.partial(main_kernel, scale), out_shape=[jax.Shap...]
where the time goes in v4:
time: 33.7 us; the launch traced here: 33.5 us
  Pallas kernels  32.9 us (98%)
  between operations  0.64 us (2%)
    pallas_call x1, Pallas kernels, main(): pl.pallas_call(functools.partial(main_kernel, scale), out_shape=[jax.Shap...  31.4 us
    pallas_call x1, Pallas kernels, finish(): pl.pallas_call(functools.partial(finish_kernel, scale), out_shape=[jax.Sh...  1.48 us

profile of v4, /device:TPU:0, one launch (start us, length us, event | category | flops | bytes accessed | tf_op | source)
XLA Modules:
  0.0 33.5 jit_solution(7250804104601843154)
XLA Ops:
  0.6 31.4 %cycle.1 = (f32[512,512]{1,0:T(8,128)S(1)}, bf16[2,4,2,2,2,64,128]{6,5,4,3,2,1,0:T(8,128)(2,1)S(1)}, bf16[2,2,256,1024]{3,2,1,0:T(8,128)(2,1)S(1)}, bf16[2,2,256...) custom-call(bf16[512,512]{1,0:T(8,128)(2,1)} %facet_hbm.1, s32[2]{0:T(128)} %ro_hbm.1, ...), custom_call_target="tpu_custom_call" | custom-call | tf_op jit(solution)/shard_map/cycle/pallas_call | solution.py:531
  32.0 1.5 %finish.1 = (f32[512,512]{1,0:T(8,128)}, f32[2,512]{1,0:T(2,128)}) custom-call(f32[512,512]{1,0:T(8,128)S(1)} %get-tuple-element.8.acc_ref, bf16[2,4,2,2,2,64,128]{6,5,4,3,2,1,0:T(8,128)(2,1)S(1)} %get-tuple-element.9.g_ref, bf16[2,2,256,1024]{3,2,1,0:T(8,128)(2,1)S(1)} %get-tuple-element.10.a_tab, bf16[2,2,256,512]{3,2,1,0:T(8,128)(2,1)S(1)} %get-tuple-element.11.bt_ref, ...), custom_call_target="tpu_custom_call" | custom-call | tf_op jit(solution)/shard_map/finish/pallas_call | solution.py:612

commit v5 on v4

--- a/solution.py
+++ b/solution.py
@@ -21,14 +21,15 @@
 LIMIT = 32 << 20
 ORDER = (
     "p:0", "rows1", "p:1", "v", "cols1",
-    "p:2", "p:3", "bt", "g:1", "r:0",
-    "r:1", "g:1", "r:2", "g:2", "x", "r:3",
-    "t:0", "t:1", "t:2", "t:3", "m",
-    "b:0", "d:1", "b:1", "d:1", "b:2", "d:2",
-    "ans", "b:3", "f:0", "own:0", "f:1", "own:1",
-    "c:0", "oth:0", "f:2", "own:2", "c:1", "oth:1",
-    "res", "f:3", "c:2", "oth:2",
-    "own:3", "c:3",
+    "p:2", "p:3", "g:0", "r:0", "bt",
+    "g:1", "r:1", "r:2", "tr", "r:3", "g:2", "r:4", "g:3",
+    "r:5", "g:4", "x", "r:6", "r:7",
+    "t:0", "t:1", "t:2", "t:3", "t:4", "t:5", "t:6", "t:7", "m",
+    "b:0", "b:1", "d:1", "b:2", "b:3", "d:1",
+    "b:4", "b:5", "d:1", "b:6", "d:1", "ans", "b:7",
+    "f:0", "f:1", "own:0", "f:2", "f:3", "own:1", "c:0", "oth:0",
+    "f:4", "f:5", "own:2", "c:1", "oth:1", "f:6", "c:2", "oth:2",
+    "f:7", "own:3", "res", "c:3",
 )
 
 scope = jax.named_scope
@@ -86,13 +87,15 @@
     return (2 * x + h, z * ny + y)
 
 
-def hots(vis, owned, lanes):
-    n = lanes.shape[1]
-    parts = []
-    for t in range(0, vis.shape[1], n):
-        v = jnp.broadcast_to(vis[1:2, t : t + n].astype(bf16), lanes.shape)
-        parts.append(jnp.where(lanes == v, jnp.ones_like(v), jnp.zeros_like(v)))
-    return owned == vis[0:1], jnp.concatenate(parts, 1)
+def hots(cell, owned, lanes):
+    row = jnp.floor(cell * (1.0 / SG))
+    v = (cell - row * SG).astype(bf16)
+    rows, cols = [], []
+    for t in range(cell.shape[0]):
+        hot = lanes == jnp.broadcast_to(v[t : t + 1], lanes.shape)
+        cols.append(jnp.where(hot, jnp.ones_like(lanes), jnp.zeros_like(lanes)))
+        rows.append(owned == row[t : t + 1])
+    return rows, jnp.concatenate(cols, 1)
 
 
 def pairs(count, body):
@@ -108,36 +111,41 @@
     lax.fori_loop(0, count // 2, step, 0)
 
 
-def semaphores():
+def split(rows_own):
+    return 2 if rows_own >= 16 else 1
+
+
+def semaphores(waves):
     plan = {}
     total = 0
-    for at, kind in enumerate((
+    kinds = (
         "plane", "z", "back_z", "back_plane", "cross",
-        "facet", "cells", "cells_z", "sums", "model", "answers",
-    )):
-        count = 4 if at < 5 else 1
+        "facet", "cells", "cells_l", "cells_z", "sums", "model", "answers",
+    )
+    for at, kind in enumerate(kinds):
+        if kind == "back_z":
+            plan[kind] = (at,) + plan["plane"][1:]
+            continue
+        count = waves if at < 4 else (4 if kind == "cross" else 1)
         plan[kind] = (at, total, count)
         total += count
     return plan, total
 
 
-def spread_rows(g_ref, a_tab, c, w, cut):
+def spread_rows(g_ref, at_ref, c, w, cut):
     wide = g_ref.shape[-1]
-    tall = a_tab.shape[2]
-    e = w % 2
-    first = (((0,), (0,)), ((), ()))
-    g = jnp.concatenate([g_ref[c, w, :, :, p].reshape(tall, wide) for p in range(2)], 1)
-    one, two = (
-        lax.dot_general(a_tab[p, e, :, cut], g, first, preferred_element_type=f32) for p in range(2)
-    )
+    parts = g_ref.shape[1] // 4
+    tall = at_ref.shape[-1]
+    g = jnp.concatenate([g_ref[c, w * parts : (w + 1) * parts, :, :, p].reshape(tall, wide) for p in range(2)], 1)
+    one, two = (jnp.dot(at_ref[p, w % 2, cut], g, preferred_element_type=f32) for p in range(2))
     return jnp.concatenate([one[:, :wide] + two[:, wide:], one[:, wide:] - two[:, :wide]], 1)
 
 
 def main_kernel(
     scale, facet_hbm, ro_hbm, co_hbm, sub_hbm, u_hbm, v_hbm, obs_hbm,
-    acc_ref, g_ref, a_tab, bt_ref, res_ref, half_u,
+    acc_ref, g_ref, at_ref, bt_ref, res_ref, half_u,
     facet_ref, ro_ref, co_ref, sub_ref, u_ref, v_ref, obs_ref,
-    kk, ks, kcol, krow, cc, cs, rc, rs, keep_col, keep_row, p_ref, vis_all, other, z_ref, zb_ref, grid_acc, own_sum, pair_sum, got_sum, own_model, got_model, lanes,
+    kk, ks, kcol, krow, cc, cs, rc, rs, keep_col, keep_row, a_tab, p_ref, vis_all, other, z_ref, zb_ref, grid_acc, own_sum, pair_sum, got_sum, own_model, got_model, lanes,
     got, own_z, send_z, got_z, gz, model, vals, slots,
     ssem, rsem, lsem,
 ):
@@ -148,11 +156,11 @@
     fs = facet_ref.shape[0]
     nv = obs_ref.shape[1]
     rows_own = NR * SG // chips
-    hr = rows_own // 2
+    parts = split(rows_own)
+    hr = rows_own // (2 * parts)
     hlong = nz * hr
-    part = 2 * hlong
+    part = 2 * parts * hlong
     wide = SG // 2
-    waves = range(4)
     sib = (2 * x + 1 - h, lax.axis_index("fcol"))
     barrier = pltpu.get_barrier_semaphore()
 
@@ -197,7 +205,7 @@
     )):
         loads.append(pltpu.make_async_copy(src, dst, lsem.at[k]))
         loads[-1].start()
-    plan = semaphores()[0]
+    plan = semaphores(4 * parts)[0]
 
     def send(kind, w, src, dst, to):
         at, base, _ = plan[kind]
@@ -249,43 +257,58 @@
         columns(h, q)
 
     def rows_half(e):
-        compose(krow[0, e], krow[1, e], rc, rs, keep_row)
+        if e > 0:
+            compose(krow[0, e], krow[1, e], rc, rs, keep_row)
         for r in range(NR):
-            cut = slice(r * wide, (r + 1) * wide)
-            a_tab[0, e, cut], a_tab[1, e, cut] = shifted(keep_row[...], row_places, ro_ref[r])
-
+            pair = shifted(keep_row[...], row_places, ro_ref[r])
+            n = wide // parts
+            for p in range(2):
+                for i in range(parts):
+                    a_tab[p, e * parts + i, r * n : (r + 1) * n] = pair[p][i * n : (i + 1) * n]
+
+    with scope("tables"):
+        expand(0, col_places, cc, cs)
+        compose(kcol[0, 0], kcol[1, 0], cc, cs, keep_col.at[0])
+        per = SG // part
+        for e in range(2):
+            for i in range(parts * per):
+                first = (i % per) * part + (e * parts + i // per) * hlong
+                src = slice(first, first + hlong)
+                dst = slice(i * hlong, (i + 1) * hlong)
+                low = slice(wide + i * hlong, wide + (i + 1) * hlong)
+                krow[0, e, dst] = kk[src]
+                krow[0, e, low] = ks[src]
+                krow[1, e, dst] = ks[src]
+                krow[1, e, low] = -kk[src]
+        expand(0, row_places, rc, rs)
+        compose(krow[0, 0], krow[1, 0], rc, rs, keep_row)
     with scope("columns0"):
-        expand(0, col_places, cc, cs)
         loads[0].wait()
         loads[1].wait()
-        columns_half(0)
+        columns(h, 0)
     with scope("cells"):
         for copy in loads[2:6]:
             copy.wait()
         sub = sub_ref[...]
         row = (lax.rem(sub, NC) * NR + lax.div(sub, NC)) * SG + u_ref[...]
-        vis_all[z, own_xy, 0:1] = row.astype(f32)
-        vis_all[z, own_xy, 1:2] = v_ref[...].astype(f32)
-        vis_all[z, own_xy, 2:4] = obs_ref[...]
+        cell = (row * SG + v_ref[...]).astype(f32)
+        for t in range(nv // 128):
+            cut = slice(t * 128, (t + 1) * 128)
+            vis_all[z, own_xy, 0, t : t + 1] = cell[:, cut]
+            vis_all[z, own_xy, 1, t : t + 1] = obs_ref[0:1, cut]
+            vis_all[z, own_xy, 2, t : t + 1] = obs_ref[1:2, cut]
     with scope("barwait"):
         pl.semaphore_wait(barrier, len(near))
-    send("facet", 0, facet_hbm, other, sib)
     for k in range(nx * ny - 1):
         mine = vis_all.at[z, own_xy]
         send("cells", 0, mine, mine, across(k)[2])
+    for d in range(1, nz):
+        mine = vis_all.at[z, own_xy]
+        send("cells_l", 0, mine, mine, to_z(d))
+    loads[6].wait()
+    send("facet", 0, facet_ref, other, sib)
     with scope("rows0"):
-        for e in range(2):
-            for b in range(SG // part):
-                src = slice(b * part + e * hlong, b * part + (e + 1) * hlong)
-                dst = slice(b * hlong, (b + 1) * hlong)
-                low = slice(wide + b * hlong, wide + (b + 1) * hlong)
-                krow[0, e, dst] = kk[src]
-                krow[0, e, low] = ks[src]
-                krow[1, e, dst] = ks[src]
-                krow[1, e, low] = -kk[src]
-        expand(0, row_places, rc, rs)
         rows_half(0)
-    loads[6].wait()
 
     def project(ref, q, base):
         step = fs // 2
@@ -305,19 +328,22 @@
             if q == 0:
                 land("facet", 0, other)
             project(other, q, (1 - h) * fs)
-        one = jnp.dot(a_tab[0, e], p_ref[...], preferred_element_type=f32)
-        two = jnp.dot(a_tab[1, e], p_ref[...], preferred_element_type=f32)
-        zr = (one[:, :wide] - two[:, wide:]).reshape(nx, ny, hlong, wide)
-        zi = (one[:, wide:] + two[:, :wide]).reshape(nx, ny, hlong, wide)
-        z_ref[w, :, :, 0] = zr
-        z_ref[w, :, :, 1] = zi
-        zb_ref[w, :, :, 0] = zr.astype(bf16)
-        zb_ref[w, :, :, 1] = zi.astype(bf16)
-        for k in range(nx * ny - 1):
-            px, py, to = across(k)
-            send("plane", w, zb_ref.at[w, px, py], got.at[w, k], to)
-
-    owned_row = lax.broadcasted_iota(i32, (2 * rows_own, nv), 0)
+        tall = parts * nx * ny * hlong
+        one, two = (
+            jnp.dot(a_tab[p, e * parts : (e + 1) * parts].reshape(tall, 2 * fs), p_ref[...], preferred_element_type=f32)
+            for p in range(2)
+        )
+        zr = (one[:, :wide] - two[:, wide:]).reshape(parts, nx, ny, hlong, wide)
+        zi = (one[:, wide:] + two[:, :wide]).reshape(parts, nx, ny, hlong, wide)
+        for i in range(parts):
+            for p, part_z in enumerate((zr, zi)):
+                z_ref[w * parts + i, :, :, p] = part_z[i]
+                zb_ref[w * parts + i, :, :, p] = part_z[i].astype(bf16)
+            for k in range(nx * ny - 1):
+                px, py, to = across(k)
+                send("plane", w * parts + i, zb_ref.at[w * parts + i, px, py], got.at[w * parts + i, k], to)
+
+    owned_row = lax.broadcasted_iota(i32, (2 * rows_own, 128), 0)
     column = owned_row // rows_own
     column = h + column - 2 * h * column
     owned_row = owned_row % rows_own
@@ -325,19 +351,31 @@
     owned_row = (owned_row + column * (NR * SG)).astype(f32)
     lanes[...] = lax.broadcasted_iota(i32, lanes.shape, 0).astype(f32).astype(bf16)
 
-    def gridding(level):
-        def one(k):
+    def gridding(ds, ks):
+        def one(level, k):
             vis = vis_all[level, k]
-            hot_row, hot_col = hots(vis, owned_row, lanes[...])
-            parts = [vis[2:3], vis[3:4], jnp.ones_like(vis[0:1])]
-            left = jnp.concatenate([jnp.where(hot_row, t, 0.0) for t in parts], 0).astype(bf16)
+            hot_rows, hot_col = hots(vis[0], owned_row, lanes[...])
+            left = []
+            for t, hot in enumerate(hot_rows):
+                values = [vis[1, t : t + 1], vis[2, t : t + 1], jnp.ones_like(vis[0, t : t + 1])]
+                left.append(jnp.concatenate([jnp.where(hot, a, 0.0) for a in values], 0).astype(bf16))
+            left = jnp.concatenate(left, 1)
             return lax.dot_general(left, hot_col, (((1,), (1,)), ((), ())), preferred_element_type=f32)
 
-        def body(k):
-            grid_acc[0] += one(k)
-            grid_acc[1] += one(k + 1)
-
-        pairs(nx * ny, body)
+        def block(i, slot):
+            level = lax.rem(z + ds.start + i // len(ks), nz)
+            grid_acc[slot] += one(level, lax.rem(own_xy + ks.start + i % len(ks), nx * ny))
+
+        if chips <= 16:
+            for i in range(len(ds) * len(ks)):
+                block(i, i % 2)
+            return
+
+        def step(i, carry):
+            block(i, 0)
+            return carry
+
+        lax.fori_loop(0, len(ds) * len(ks), step, 0)
 
     def reduce(w):
         land("plane", w, got.at[w])
@@ -353,7 +391,7 @@
             send("z", w, send_z.at[w, lax.rem(z + d, nz)], got_z.at[w, d - 1], to_z(d))
 
     def turn(w):
-        q, e = w // 2, w % 2
+        q, e = w // (2 * parts), w % (2 * parts)
         if w == 0:
             land("sums", 0, got_sum)
         land("z", w, got_z.at[w])
@@ -375,7 +413,7 @@
 
     def over(w, px, py):
         src = g_ref.at[h, w, px, py]
-        send("cross", w, src, src, sib)
+        send("cross", w // parts, src, src, sib)
 
     def gather(w):
         land("back_z", w, gz.at[w, : nz - 1])
@@ -395,21 +433,25 @@
             over(w, px, py)
 
     def crossed(w):
-        land("cross", w, g_ref.at[1 - h, w])
+        land("cross", w, g_ref.at[1 - h, w * parts : (w + 1) * parts])
 
     def degrid(level):
         m = jnp.concatenate([own_model[...], got_model[...]], 0)
 
         def one(k):
-            hot_row, hot_col = hots(vis_all[level, k], owned_row, lanes[...])
+            hot_rows, hot_col = hots(vis_all[level, k][0], owned_row, lanes[...])
             val = jnp.dot(m, hot_col, preferred_element_type=f32)
             out = []
             for p in range(2):
-                picked = [
-                    jnp.where(hot_row[c * rows_own : (c + 1) * rows_own], val[(2 * c + p) * rows_own : (2 * c + p + 1) * rows_own], 0.0)
-                    for c in range(2)
-                ]
-                out.append(jnp.sum(picked[0] + picked[1], 0, keepdims=True))
+                line = []
+                for t, hot in enumerate(hot_rows):
+                    cut = slice(t * 128, (t + 1) * 128)
+                    picked = [
+                        jnp.where(hot[c * rows_own : (c + 1) * rows_own], val[(2 * c + p) * rows_own : (2 * c + p + 1) * rows_own, cut], 0.0)
+                        for c in range(2)
+                    ]
+                    line.append(jnp.sum(picked[0] + picked[1], 0, keepdims=True))
+                out.append(jnp.concatenate(line, 1))
             return jnp.concatenate(out, 0)
 
         def body(k):
@@ -423,7 +465,7 @@
     def image(side, w):
         c = h if side == 0 else 1 - h
         q, e = w // 2, w % 2
-        u = spread_rows(g_ref, a_tab, c, w, own_cut)
+        u = spread_rows(g_ref, at_ref, c, w, slice(None))
         if e == 0:
             half_u[side] = u
             return
@@ -435,16 +477,19 @@
             acc_ref[...] += got
 
     grid_acc[...] = jnp.zeros_like(grid_acc)
-    done = {"grid": 0, "degrid": 0}
-
-    def grid(n):
-        for _ in range(n * nz // 4):
-            k = done["grid"]
-            done["grid"] += 1
-            if k == 1:
-                land("cells_z", 0, vis_all.at[: nz - 1])
-            with scope("grid%d" % k):
-                gridding(lax.rem(z + k, nz))
+    done = {"degrid": 0}
+
+    def grid(k):
+        if k == 0:
+            gridding(range(0, 1), range(0, nx * ny))
+        elif k == 1:
+            land("cells_l", 0, vis_all.at[: nz - 1, own_xy])
+            gridding(range(1, nz), range(0, 1))
+        else:
+            if k == 2:
+                land("cells_z", 0, vis_all.at[: nz - 1, : nx * ny - 1])
+            last = nz if k == 4 else k
+            gridding(range(k - 1, last), range(1, nx * ny))
 
     def exchange():
         for p in range(3):
@@ -469,9 +514,10 @@
 
     def cells():
         land("cells", 0, vis_all.at[z, : nx * ny - 1])
-        sheet = vis_all.at[z]
-        for d in range(1, nz):
-            send("cells_z", 0, sheet, sheet, to_z(d))
+        for k in range(1, nx * ny):
+            block = vis_all.at[z, lax.rem(own_xy + k, nx * ny)]
+            for d in range(1, nz):
+                send("cells_z", 0, block, block, to_z(d))
 
     def answers():
         peers(lambda pz, pxy, slot, to: send("answers", 0, vals.at[pz, pxy], slots.at[me], to))
@@ -487,32 +533,38 @@
                 total = total + slots[lax.rem(me + d, chips)]
         res_ref[...] = obs_ref[...] - total
 
+    def turned():
+        for p in range(2):
+            for e in range(2):
+                block = a_tab[p, e * parts : (e + 1) * parts, :, own_cut].reshape(at_ref.shape[-1], fs)
+                at_ref[p, e] = block.T
+
     def late_columns():
         columns(1 - h, 0)
         columns(1 - h, 1)
 
     acts = {
-        "p": produce, "r": reduce, "t": turn, "b": gather, "f": finish, "c": crossed,
+        "p": produce, "g": grid, "r": reduce, "t": turn, "b": gather, "f": finish, "c": crossed,
         "own": lambda w: image(0, w), "oth": lambda w: image(1, w),
     }
     simple = {
-        "v": cells, "ans": answers, "res": result, "x": exchange, "m": models,
+        "v": cells, "ans": answers, "res": result, "x": exchange, "m": models, "tr": turned,
         "rows1": lambda: rows_half(1), "cols1": lambda: columns_half(1), "bt": late_columns,
     }
     for word in ORDER:
         name, _, arg = word.partition(":")
-        if name == "g":
-            grid(int(arg))
-        elif name == "d":
+        if name == "d":
             ungrid(int(arg))
         else:
+            if name in ("r", "t", "b", "f") and int(arg) >= 4 * parts:
+                continue
             with scope(name + arg):
                 acts[name](int(arg)) if arg else simple[name]()
     with scope("drain"):
         for kind, like in (
             ("plane", got), ("z", got_z), ("back_z", got_z), ("back_plane", got),
             ("cross", g_ref.at[h]), ("facet", other), ("cells", vis_all.at[z, : nx * ny - 1]),
-            ("cells_z", vis_all.at[: nz - 1]), ("sums", got_sum), ("model", got_model), ("answers", slots.at[: chips - 1]),
+            ("cells_l", vis_all.at[: nz - 1, own_xy]), ("cells_z", vis_all.at[: nz - 1, : nx * ny - 1]), ("sums", got_sum), ("model", got_model), ("answers", slots.at[: chips - 1]),
         ):
             sentall(kind, like)
 
@@ -523,17 +575,19 @@
     fs = facet.shape[0]
     nv = obs.shape[1]
     rows_own = NR * SG // chips
-    hr = rows_own // 2
+    parts = split(rows_own)
+    waves = 4 * parts
+    hr = rows_own // (2 * parts)
     hlong = nz * hr
     wide = SG // 2
-    plan, total = semaphores()
+    plan, total = semaphores(waves)
     dma = pltpu.SemaphoreType.DMA
     return pl.pallas_call(
         functools.partial(main_kernel, scale),
         out_shape=[
             jax.ShapeDtypeStruct((fs, fs), f32),
-            jax.ShapeDtypeStruct((2, 4, nx, ny, 2, hlong, wide), bf16),
-            jax.ShapeDtypeStruct((2, 2, nx * ny * hlong, 2 * fs), bf16),
+            jax.ShapeDtypeStruct((2, waves, nx, ny, 2, hlong, wide), bf16),
+            jax.ShapeDtypeStruct((2, 2, fs, parts * nx * ny * hlong), bf16),
             jax.ShapeDtypeStruct((NC, 2, SG, fs), bf16),
             jax.ShapeDtypeStruct((2, nv), f32),
             jax.ShapeDtypeStruct((2, fs, SG), f32),
@@ -558,11 +612,12 @@
             pltpu.VMEM((SG, 2 * fs), bf16),
             pltpu.VMEM((2, SG, fs), f32),
             pltpu.VMEM((SG, 2 * fs), f32),
+            pltpu.VMEM((2, 2 * parts, nx * ny * hlong, 2 * fs), bf16),
             pltpu.VMEM((2 * fs, SG), bf16),
-            pltpu.VMEM((nz, nx * ny, 4, nv), f32),
+            pltpu.VMEM((nz, nx * ny, 3, nv // 128, 128), f32),
             pltpu.VMEM((fs, fs), bf16),
-            pltpu.VMEM((4, nx, ny, 2, hlong, wide), f32),
-            pltpu.VMEM((4, nx, ny, 2, hlong, wide), bf16),
+            pltpu.VMEM((waves, nx, ny, 2, hlong, wide), f32),
+            pltpu.VMEM((waves, nx, ny, 2, hlong, wide), bf16),
             pltpu.VMEM((2, 6 * rows_own, SG), f32),
             pltpu.VMEM((3, rows_own, SG), f32),
             pltpu.VMEM((3, rows_own, SG), f32),
@@ -570,11 +625,11 @@
             pltpu.VMEM((2 * rows_own, SG), bf16),
             pltpu.VMEM((2 * rows_own, SG), bf16),
             pltpu.VMEM((SG, 128), bf16),
-            pltpu.VMEM((4, nx * ny - 1, 2, hlong, wide), bf16),
-            pltpu.VMEM((4, nz, hr, SG), f32),
-            pltpu.VMEM((4, nz, hr, SG), bf16),
-            pltpu.VMEM((4, nz - 1, hr, SG), bf16),
-            pltpu.VMEM((4, nz, hr, SG), bf16),
+            pltpu.VMEM((waves, nx * ny - 1, 2, hlong, wide), bf16),
+            pltpu.VMEM((waves, nz, hr, SG), f32),
+            pltpu.VMEM((waves, nz, hr, SG), bf16),
+            pltpu.VMEM((waves, nz - 1, hr, SG), bf16),
+            pltpu.VMEM((waves, nz, hr, SG), bf16),
             pltpu.VMEM((2 * rows_own, SG), f32),
             pltpu.VMEM((nz, nx * ny, 2, nv), f32),
             pltpu.VMEM((chips, 2, nv), f32),
@@ -589,7 +644,7 @@
     )(*(pltpu.with_memory_space_constraint(a, pltpu.HBM) for a in (facet, ro, co, sub, u, v, obs)))
 
 
-def finish_kernel(scale, acc_ref, g_ref, a_tab, bt_ref, res_ref, half_u, image_hbm, out_hbm, buf, sem):
+def finish_kernel(scale, acc_ref, g_ref, at_ref, bt_ref, res_ref, half_u, image_hbm, out_hbm, buf, sem):
     _, h, _, _ = position()
     fs = acc_ref.shape[0]
     pieces = sem.shape[0] - 1
@@ -598,7 +653,7 @@
     copies[0].start()
     for k in range(pieces):
         cut = slice(k * step, (k + 1) * step)
-        u = spread_rows(g_ref, a_tab, 1 - h, 3, pl.ds(pl.multiple_of(h * fs + k * step, step), step))
+        u = spread_rows(g_ref, at_ref, 1 - h, 3, cut)
         u = (half_u[1, cut] + u).astype(bf16)
         buf[cut] = (acc_ref[cut] + jnp.dot(u, bt_ref[1 - h, 1], preferred_element_type=f32)) * scale
         copies.append(pltpu.make_async_copy(buf.at[cut], image_hbm.at[cut], sem.at[k]))

time: 33.7 us -> 32.4 us (0.961)
  Pallas kernels: 32.9 us -> 31.6 us
    pallas_call x1, Pallas kernels: 31.4 us -> 30.2 us  [main(): pl.pallas_call(functools.partial(main_kernel, scale), out_shape=[jax.Shap...]
where the time goes in v5:
time: 32.4 us; the launch traced here: 32.2 us
  Pallas kernels  31.6 us (98%)
  between operations  0.64 us (2%)
    pallas_call x1, Pallas kernels, main(): pl.pallas_call(functools.partial(main_kernel, scale), out_shape=[jax.Shap...  30.2 us
    pallas_call x1, Pallas kernels, finish(): pl.pallas_call(functools.partial(finish_kernel, scale), out_shape=[jax.Sh...  1.43 us

profile of v5, /device:TPU:0, one launch (start us, length us, event | category | flops | bytes accessed | tf_op | source)
XLA Modules:
  0.0 32.2 jit_solution(1980982107778507452)
XLA Ops:
  0.6 30.2 %cycle.1 = (f32[512,512]{1,0:T(8,128)S(1)}, bf16[2,8,2,2,2,32,128]{6,5,4,3,2,1,0:T(8,128)(2,1)S(1)}, bf16[2,2,512,256]{3,2,1,0:T(8,128)(2,1)S(1)}, bf16[2,2,256,...) custom-call(bf16[512,512]{1,0:T(8,128)(2,1)} %facet_hbm.1, s32[2]{0:T(128)} %ro_hbm.1, ...), custom_call_target="tpu_custom_call" | custom-call | tf_op jit(solution)/shard_map/cycle/pallas_call | solution.py:585
  30.8 1.4 %finish.1 = (f32[512,512]{1,0:T(8,128)}, f32[2,512]{1,0:T(2,128)}) custom-call(f32[512,512]{1,0:T(8,128)S(1)} %get-tuple-element.8.acc_ref, bf16[2,8,2,2,2,32,128]{6,5,4,3,2,1,0:T(8,128)(2,1)S(1)} %get-tuple-element.9.g_ref, bf16[2,2,512,256]{3,2,1,0:T(8,128)(2,1)S(1)} %get-tuple-element.10.at_ref, bf16[2,2,256,512]{3,2,1,0:T(8,128)(2,1)S(1)} %get-tuple-element.11.bt_ref, ...), custom_call_target="tpu_custom_call" | custom-call | tf_op jit(solution)/shard_map/finish/pallas_call | solution.py:667

commit v6 on v5

--- a/solution.py
+++ b/solution.py
@@ -21,12 +21,11 @@
 LIMIT = 32 << 20
 ORDER = (
     "p:0", "rows1", "p:1", "v", "cols1",
-    "p:2", "p:3", "g:0", "r:0", "bt",
-    "g:1", "r:1", "r:2", "tr", "r:3", "g:2", "r:4", "g:3",
-    "r:5", "g:4", "x", "r:6", "r:7",
-    "t:0", "t:1", "t:2", "t:3", "t:4", "t:5", "t:6", "t:7", "m",
-    "b:0", "b:1", "d:1", "b:2", "b:3", "d:1",
-    "b:4", "b:5", "d:1", "b:6", "d:1", "ans", "b:7",
+    "p:2", "p:3", "r:0", "g:0", "r:1", "g:1",
+    "r:2", "g:2", "r:3", "g:3", "r:4", "g:4", "x", "r:5", "bt", "r:6", "tr", "r:7",
+    "t:0", "t:1", "t:2", "t:3", "t:4", "t:5", "b:0", "t:6", "t:7", "m", "b:1",
+    "b:2", "b:3", "d:1", "b:4", "d:1",
+    "b:5", "d:1", "b:6", "d:1", "ans", "b:7",
     "f:0", "f:1", "own:0", "f:2", "f:3", "own:1", "c:0", "oth:0",
     "f:4", "f:5", "own:2", "c:1", "oth:1", "f:6", "c:2", "oth:2",
     "f:7", "own:3", "res", "c:3",
@@ -143,7 +142,7 @@
 
 def main_kernel(
     scale, facet_hbm, ro_hbm, co_hbm, sub_hbm, u_hbm, v_hbm, obs_hbm,
-    acc_ref, g_ref, at_ref, bt_ref, res_ref, half_u,
+    acc_ref, g_ref, at_ref, bt_ref, res_ref, half_u, full_u,
     facet_ref, ro_ref, co_ref, sub_ref, u_ref, v_ref, obs_ref,
     kk, ks, kcol, krow, cc, cs, rc, rs, keep_col, keep_row, a_tab, p_ref, vis_all, other, z_ref, zb_ref, grid_acc, own_sum, pair_sum, got_sum, own_model, got_model, lanes,
     got, own_z, send_z, got_z, gz, model, vals, slots,
@@ -470,11 +469,12 @@
             half_u[side] = u
             return
         total = (half_u[side] + u).astype(bf16)
-        got = jnp.dot(total, bt_ref[c, q], preferred_element_type=f32)
-        if q == 0 and side == 0:
-            acc_ref[...] = got
-        else:
-            acc_ref[...] += got
+        if side == 0:
+            full_u[...] = total
+            return
+        acc_ref[...] = jnp.dot(full_u[...], bt_ref[h, q], preferred_element_type=f32) + jnp.dot(
+            total, bt_ref[1 - h, q], preferred_element_type=f32
+        )
 
     grid_acc[...] = jnp.zeros_like(grid_acc)
     done = {"degrid": 0}
@@ -591,9 +591,10 @@
             jax.ShapeDtypeStruct((NC, 2, SG, fs), bf16),
             jax.ShapeDtypeStruct((2, nv), f32),
             jax.ShapeDtypeStruct((2, fs, SG), f32),
+            jax.ShapeDtypeStruct((fs, SG), bf16),
         ],
         in_specs=[HB] * 7,
-        out_specs=[VM] * 6,
+        out_specs=[VM] * 7,
         scratch_shapes=[
             pltpu.VMEM((fs, fs), bf16),
             pltpu.SMEM((NR,), i32),
@@ -644,35 +645,41 @@
     )(*(pltpu.with_memory_space_constraint(a, pltpu.HBM) for a in (facet, ro, co, sub, u, v, obs)))
 
 
-def finish_kernel(scale, acc_ref, g_ref, at_ref, bt_ref, res_ref, half_u, image_hbm, out_hbm, buf, sem):
+def finish_kernel(
+    scale, acc_ref, g_ref, at_ref, bt_ref, res_ref, half_u, full_u, image_hbm, out_hbm, buf, sem
+):
     _, h, _, _ = position()
     fs = acc_ref.shape[0]
-    pieces = sem.shape[0] - 1
+    pieces, each = 2, 2
     step = fs // pieces
-    copies = [pltpu.make_async_copy(res_ref, out_hbm, sem.at[pieces])]
+    copies = [pltpu.make_async_copy(res_ref, out_hbm, sem.at[pieces * each])]
     copies[0].start()
     for k in range(pieces):
         cut = slice(k * step, (k + 1) * step)
-        u = spread_rows(g_ref, at_ref, 1 - h, 3, cut)
-        u = (half_u[1, cut] + u).astype(bf16)
-        buf[cut] = (acc_ref[cut] + jnp.dot(u, bt_ref[1 - h, 1], preferred_element_type=f32)) * scale
-        copies.append(pltpu.make_async_copy(buf.at[cut], image_hbm.at[cut], sem.at[k]))
-        copies[-1].start()
+        u = (half_u[1, cut] + spread_rows(g_ref, at_ref, 1 - h, 3, cut)).astype(bf16)
+        got = jnp.dot(full_u[cut], bt_ref[h, 1], preferred_element_type=f32)
+        got += jnp.dot(u, bt_ref[1 - h, 1], preferred_element_type=f32)
+        buf[cut] = (acc_ref[cut] + got) * scale
+        for i in range(each):
+            row = k * step + i * (step // each)
+            rows = slice(row, row + step // each)
+            copies.append(pltpu.make_async_copy(buf.at[rows], image_hbm.at[rows], sem.at[k * each + i]))
+            copies[-1].start()
     for copy in copies:
         copy.wait()
 
 
-def finish(acc, g, a_tab, bt, res, u, scale):
+def finish(acc, g, at, bt, res, half_u, full_u, scale):
     fs = acc.shape[0]
     return pl.pallas_call(
         functools.partial(finish_kernel, scale),
         out_shape=[jax.ShapeDtypeStruct((fs, fs), f32), jax.ShapeDtypeStruct(res.shape, f32)],
-        in_specs=[VM] * 6,
+        in_specs=[VM] * 7,
         out_specs=[HB] * 2,
-        scratch_shapes=[pltpu.VMEM((fs, fs), f32), pltpu.SemaphoreType.DMA((3,))],
+        scratch_shapes=[pltpu.VMEM((fs, fs), f32), pltpu.SemaphoreType.DMA((5,))],
         compiler_params=pltpu.CompilerParams(vmem_limit_bytes=6 << 20),
         name="finish",
-    )(acc, g, a_tab, bt, res, u)
+    )(acc, g, at, bt, res, half_u, full_u)
 
 
 def shards(facet_image, row_offsets, col_offsets, vis_subgrid, vis_u, vis_v, observed):
@@ -680,11 +687,11 @@
     fs = facet_image.shape[0]
     scale_in = 1.0 / (fs * math.sqrt(rows * cols))
     scale_out = 1.0 / (SG * math.sqrt(NR * NC))
-    acc, g, a_tab, bt, residual, u = main(
+    acc, g, at, bt, residual, half_u, full_u = main(
         row_offsets, col_offsets, vis_subgrid[None], vis_u[None], vis_v[None],
         observed, facet_image, scale_in / SG,
     )
-    return tuple(finish(acc, g, a_tab, bt, residual, u, scale_out / SG))
+    return tuple(finish(acc, g, at, bt, residual, half_u, full_u, scale_out / SG))
 
 
 def solution(mesh):

time: 32.4 us -> 31.3 us (0.966)
  Pallas kernels: 31.6 us -> 30.5 us
    pallas_call x1, Pallas kernels: 30.2 us -> 28.9 us  [main(): pl.pallas_call(functools.partial(main_kernel, scale), out_shape=[jax.Shap...]
where the time goes in v6:
time: 31.3 us; the launch traced here: 31.1 us
  Pallas kernels  30.5 us (97%)
  between operations  0.64 us (2%)
    pallas_call x1, Pallas kernels, main(): pl.pallas_call(functools.partial(main_kernel, scale), out_shape=[jax.Shap...  28.9 us
    pallas_call x1, Pallas kernels, finish(): pl.pallas_call(functools.partial(finish_kernel, scale), out_shape=[jax.Sh...  1.58 us

profile of v6, /device:TPU:0, one launch (start us, length us, event | category | flops | bytes accessed | tf_op | source)
XLA Modules:
  0.0 31.1 jit_solution(10017499699203847953)
XLA Ops:
  0.6 28.9 %cycle.1 = (f32[512,512]{1,0:T(8,128)S(1)}, bf16[2,8,2,2,2,32,128]{6,5,4,3,2,1,0:T(8,128)(2,1)S(1)}, bf16[2,2,512,256]{3,2,1,0:T(8,128)(2,1)S(1)}, bf16[2,2,256,...) custom-call(bf16[512,512]{1,0:T(8,128)(2,1)} %facet_hbm.1, ...), custom_call_target="tpu_custom_call" | custom-call | tf_op jit(solution)/shard_map/cycle/pallas_call | solution.py:585
  29.5 1.6 %finish.1 = (f32[512,512]{1,0:T(8,128)}, f32[2,512]{1,0:T(2,128)}) custom-call(f32[512,512]{1,0:T(8,128)S(1)} %get-tuple-element.9.acc_ref, bf16[2,8,2,2,2,32,128]{6,5,4,3,2,1,0:T(8,128)(2,1)S(1)} %get-tuple-element.10.g_ref, bf16[2,2,512,256]{3,2,1,0:T(8,128)(2,1)S(1)} %get-tuple-element.11.at_ref, bf16[2,2,256,512]{3,2,1,0:T(8,128)(2,1)S(1)} %get-tuple-element.12.bt_ref, ...), custom_call_target="tpu_custom_call" | custom-call | tf_op jit(solution)/shard_map/finish/pallas_call | solution.py:674

commit v7 on v6

--- a/solution.py
+++ b/solution.py
@@ -25,10 +25,10 @@
     "r:2", "g:2", "r:3", "g:3", "r:4", "g:4", "x", "r:5", "bt", "r:6", "tr", "r:7",
     "t:0", "t:1", "t:2", "t:3", "t:4", "t:5", "b:0", "t:6", "t:7", "m", "b:1",
     "b:2", "b:3", "d:1", "b:4", "d:1",
-    "b:5", "d:1", "b:6", "d:1", "ans", "b:7",
+    "b:5", "d:1", "b:6", "b:7", "d:1", "ans",
     "f:0", "f:1", "own:0", "f:2", "f:3", "own:1", "c:0", "oth:0",
     "f:4", "f:5", "own:2", "c:1", "oth:1", "f:6", "c:2", "oth:2",
-    "f:7", "own:3", "res", "c:3",
+    "f:7", "own:3", "fin", "res", "c:3",
 )
 
 scope = jax.named_scope
@@ -142,8 +142,8 @@
 
 def main_kernel(
     scale, facet_hbm, ro_hbm, co_hbm, sub_hbm, u_hbm, v_hbm, obs_hbm,
-    acc_ref, g_ref, at_ref, bt_ref, res_ref, half_u, full_u,
-    facet_ref, ro_ref, co_ref, sub_ref, u_ref, v_ref, obs_ref,
+    acc_ref, g_ref, at_ref, bt_ref, res_ref, half_u,
+    full_u, facet_ref, ro_ref, co_ref, sub_ref, u_ref, v_ref, obs_ref,
     kk, ks, kcol, krow, cc, cs, rc, rs, keep_col, keep_row, a_tab, p_ref, vis_all, other, z_ref, zb_ref, grid_acc, own_sum, pair_sum, got_sum, own_model, got_model, lanes,
     got, own_z, send_z, got_z, gz, model, vals, slots,
     ssem, rsem, lsem,
@@ -456,8 +456,8 @@
         def body(k):
             a = one(k)
             b = one(k + 1)
-            vals[level, k] = a
-            vals[level, k + 1] = b
+            vals[level, k] = a.astype(bf16)
+            vals[level, k + 1] = b.astype(bf16)
 
         pairs(nx * ny, body)
 
@@ -524,13 +524,13 @@
 
     def result():
         land("answers", 0, slots.at[: chips - 1])
-        start = vals[z, own_xy]
+        start = vals[z, own_xy].astype(f32)
         if chips > 16:
-            total = lax.fori_loop(1, chips, lambda d, t: t + slots[lax.rem(me + d, chips)], start)
+            total = lax.fori_loop(1, chips, lambda d, t: t + slots[lax.rem(me + d, chips)].astype(f32), start)
         else:
             total = start
             for d in range(1, chips):
-                total = total + slots[lax.rem(me + d, chips)]
+                total = total + slots[lax.rem(me + d, chips)].astype(f32)
         res_ref[...] = obs_ref[...] - total
 
     def turned():
@@ -543,12 +543,15 @@
         columns(1 - h, 0)
         columns(1 - h, 1)
 
+    def own_last():
+        acc_ref[...] += jnp.dot(full_u[...], bt_ref[h, 1], preferred_element_type=f32)
+
     acts = {
         "p": produce, "g": grid, "r": reduce, "t": turn, "b": gather, "f": finish, "c": crossed,
         "own": lambda w: image(0, w), "oth": lambda w: image(1, w),
     }
     simple = {
-        "v": cells, "ans": answers, "res": result, "x": exchange, "m": models, "tr": turned,
+        "v": cells, "ans": answers, "res": result, "x": exchange, "fin": own_last, "m": models, "tr": turned,
         "rows1": lambda: rows_half(1), "cols1": lambda: columns_half(1), "bt": late_columns,
     }
     for word in ORDER:
@@ -591,11 +594,11 @@
             jax.ShapeDtypeStruct((NC, 2, SG, fs), bf16),
             jax.ShapeDtypeStruct((2, nv), f32),
             jax.ShapeDtypeStruct((2, fs, SG), f32),
-            jax.ShapeDtypeStruct((fs, SG), bf16),
         ],
         in_specs=[HB] * 7,
-        out_specs=[VM] * 7,
+        out_specs=[VM] * 6,
         scratch_shapes=[
+            pltpu.VMEM((fs, SG), bf16),
             pltpu.VMEM((fs, fs), bf16),
             pltpu.SMEM((NR,), i32),
             pltpu.SMEM((NC,), i32),
@@ -632,8 +635,8 @@
             pltpu.VMEM((waves, nz - 1, hr, SG), bf16),
             pltpu.VMEM((waves, nz, hr, SG), bf16),
             pltpu.VMEM((2 * rows_own, SG), f32),
-            pltpu.VMEM((nz, nx * ny, 2, nv), f32),
-            pltpu.VMEM((chips, 2, nv), f32),
+            pltpu.VMEM((nz, nx * ny, 2, nv), bf16),
+            pltpu.VMEM((chips, 2, nv), bf16),
             dma((len(plan),)),
             dma((total,)),
             dma((8,)),
@@ -646,7 +649,7 @@
 
 
 def finish_kernel(
-    scale, acc_ref, g_ref, at_ref, bt_ref, res_ref, half_u, full_u, image_hbm, out_hbm, buf, sem
+    scale, acc_ref, g_ref, at_ref, bt_ref, res_ref, half_u, image_hbm, out_hbm, buf, sem
 ):
     _, h, _, _ = position()
     fs = acc_ref.shape[0]
@@ -657,8 +660,7 @@
     for k in range(pieces):
         cut = slice(k * step, (k + 1) * step)
         u = (half_u[1, cut] + spread_rows(g_ref, at_ref, 1 - h, 3, cut)).astype(bf16)
-        got = jnp.dot(full_u[cut], bt_ref[h, 1], preferred_element_type=f32)
-        got += jnp.dot(u, bt_ref[1 - h, 1], preferred_element_type=f32)
+        got = jnp.dot(u, bt_ref[1 - h, 1], preferred_element_type=f32)
         buf[cut] = (acc_ref[cut] + got) * scale
         for i in range(each):
             row = k * step + i * (step // each)
@@ -669,17 +671,17 @@
         copy.wait()
 
 
-def finish(acc, g, at, bt, res, half_u, full_u, scale):
+def finish(acc, g, at, bt, res, half_u, scale):
     fs = acc.shape[0]
     return pl.pallas_call(
         functools.partial(finish_kernel, scale),
         out_shape=[jax.ShapeDtypeStruct((fs, fs), f32), jax.ShapeDtypeStruct(res.shape, f32)],
-        in_specs=[VM] * 7,
+        in_specs=[VM] * 6,
         out_specs=[HB] * 2,
         scratch_shapes=[pltpu.VMEM((fs, fs), f32), pltpu.SemaphoreType.DMA((5,))],
         compiler_params=pltpu.CompilerParams(vmem_limit_bytes=6 << 20),
         name="finish",
-    )(acc, g, at, bt, res, half_u, full_u)
+    )(acc, g, at, bt, res, half_u)
 
 
 def shards(facet_image, row_offsets, col_offsets, vis_subgrid, vis_u, vis_v, observed):
@@ -687,11 +689,11 @@
     fs = facet_image.shape[0]
     scale_in = 1.0 / (fs * math.sqrt(rows * cols))
     scale_out = 1.0 / (SG * math.sqrt(NR * NC))
-    acc, g, at, bt, residual, half_u, full_u = main(
+    acc, g, at, bt, residual, half_u = main(
         row_offsets, col_offsets, vis_subgrid[None], vis_u[None], vis_v[None],
         observed, facet_image, scale_in / SG,
     )
-    return tuple(finish(acc, g, at, bt, residual, half_u, full_u, scale_out / SG))
+    return tuple(finish(acc, g, at, bt, residual, half_u, scale_out / SG))
 
 
 def solution(mesh):

time: 31.3 us -> 31.1 us (level)
  no operation moved by 1% of the time
where the time goes in v7:
time: 31.1 us; the launch traced here: 30.9 us
  Pallas kernels  30.3 us (97%)
  between operations  0.64 us (2%)
    pallas_call x1, Pallas kernels, main(): pl.pallas_call(functools.partial(main_kernel, scale), out_shape=[jax.Shap...  28.8 us
    pallas_call x1, Pallas kernels, finish(): pl.pallas_call(functools.partial(finish_kernel, scale), out_shape=[jax.Sh...  1.44 us

profile of v7, /device:TPU:0, one launch (start us, length us, event | category | flops | bytes accessed | tf_op | source)
XLA Modules:
  0.0 30.9 jit_solution(13320585134844992699)
XLA Ops:
  0.6 28.8 %cycle.1 = (f32[512,512]{1,0:T(8,128)S(1)}, bf16[2,8,2,2,2,32,128]{6,5,4,3,2,1,0:T(8,128)(2,1)S(1)}, bf16[2,2,512,256]{3,2,1,0:T(8,128)(2,1)S(1)}, bf16[2,2,256,...) custom-call(bf16[512,512]{1,0:T(8,128)(2,1)} %facet_hbm.1, s32[2]{0:T(128)} %ro_hbm.1, ...), custom_call_target="tpu_custom_call" | custom-call | tf_op jit(solution)/shard_map/cycle/pallas_call | solution.py:588
  29.5 1.4 %finish.1 = (f32[512,512]{1,0:T(8,128)}, f32[2,512]{1,0:T(2,128)}) custom-call(f32[512,512]{1,0:T(8,128)S(1)} %get-tuple-element.8.acc_ref, bf16[2,8,2,2,2,32,128]{6,5,4,3,2,1,0:T(8,128)(2,1)S(1)} %get-tuple-element.9.g_ref, bf16[2,2,512,256]{3,2,1,0:T(8,128)(2,1)S(1)} %get-tuple-element.10.at_ref, bf16[2,2,256,512]{3,2,1,0:T(8,128)(2,1)S(1)} %get-tuple-element.11.bt_ref, ...), custom_call_target="tpu_custom_call" | custom-call | tf_op jit(solution)/shard_map/finish/pallas_call | solution.py:676

commit v8 on v7

--- a/solution.py
+++ b/solution.py
@@ -639,7 +639,7 @@
             pltpu.VMEM((chips, 2, nv), bf16),
             dma((len(plan),)),
             dma((total,)),
-            dma((8,)),
+            dma((7,)),
         ],
         compiler_params=pltpu.CompilerParams(
             collective_id=0, has_side_effects=True, vmem_limit_bytes=LIMIT
@@ -653,20 +653,17 @@
 ):
     _, h, _, _ = position()
     fs = acc_ref.shape[0]
-    pieces, each = 2, 2
-    step = fs // pieces
-    copies = [pltpu.make_async_copy(res_ref, out_hbm, sem.at[pieces * each])]
+    edges = (0, fs * 5 // 8, fs)
+    pieces = len(edges) - 1
+    copies = [pltpu.make_async_copy(res_ref, out_hbm, sem.at[pieces])]
     copies[0].start()
     for k in range(pieces):
-        cut = slice(k * step, (k + 1) * step)
+        cut = slice(edges[k], edges[k + 1])
         u = (half_u[1, cut] + spread_rows(g_ref, at_ref, 1 - h, 3, cut)).astype(bf16)
         got = jnp.dot(u, bt_ref[1 - h, 1], preferred_element_type=f32)
         buf[cut] = (acc_ref[cut] + got) * scale
-        for i in range(each):
-            row = k * step + i * (step // each)
-            rows = slice(row, row + step // each)
-            copies.append(pltpu.make_async_copy(buf.at[rows], image_hbm.at[rows], sem.at[k * each + i]))
-            copies[-1].start()
+        copies.append(pltpu.make_async_copy(buf.at[cut], image_hbm.at[cut], sem.at[k]))
+        copies[-1].start()
     for copy in copies:
         copy.wait()
 
@@ -678,7 +675,7 @@
         out_shape=[jax.ShapeDtypeStruct((fs, fs), f32), jax.ShapeDtypeStruct(res.shape, f32)],
         in_specs=[VM] * 6,
         out_specs=[HB] * 2,
-        scratch_shapes=[pltpu.VMEM((fs, fs), f32), pltpu.SemaphoreType.DMA((5,))],
+        scratch_shapes=[pltpu.VMEM((fs, fs), f32), pltpu.SemaphoreType.DMA((3,))],
         compiler_params=pltpu.CompilerParams(vmem_limit_bytes=6 << 20),
         name="finish",
     )(acc, g, at, bt, res, half_u)

time: 31.1 us -> 31 us (level)
  no operation moved by 1% of the time
where the time goes in v8:
time: 31 us; the launch traced here: 30.8 us
  Pallas kernels  30.2 us (97%)
  between operations  0.64 us (2%)
    pallas_call x1, Pallas kernels, main(): pl.pallas_call(functools.partial(main_kernel, scale), out_shape=[jax.Shap...  28.8 us
    pallas_call x1, Pallas kernels, finish(): pl.pallas_call(functools.partial(finish_kernel, scale), out_shape=[jax.Sh...  1.4 us

profile of v8, /device:TPU:0, one launch (start us, length us, event | category | flops | bytes accessed | tf_op | source)
XLA Modules:
  0.0 30.8 jit_solution(5830939142087098727)
XLA Ops:
  0.6 28.8 %cycle.1 = (f32[512,512]{1,0:T(8,128)S(1)}, bf16[2,8,2,2,2,32,128]{6,5,4,3,2,1,0:T(8,128)(2,1)S(1)}, bf16[2,2,512,256]{3,2,1,0:T(8,128)(2,1)S(1)}, bf16[2,2,256,...) custom-call(bf16[512,512]{1,0:T(8,128)(2,1)} %facet_hbm.1, s32[2]{0:T(128)} %ro_hbm.1, ...), custom_call_target="tpu_custom_call" | custom-call | tf_op jit(solution)/shard_map/cycle/pallas_call | solution.py:588
  29.5 1.4 %finish.1 = (f32[512,512]{1,0:T(8,128)}, f32[2,512]{1,0:T(2,128)}) custom-call(f32[512,512]{1,0:T(8,128)S(1)} %get-tuple-element.8.acc_ref, bf16[2,8,2,2,2,32,128]{6,5,4,3,2,1,0:T(8,128)(2,1)S(1)} %get-tuple-element.9.g_ref, bf16[2,2,512,256]{3,2,1,0:T(8,128)(2,1)S(1)} %get-tuple-element.10.at_ref, bf16[2,2,256,512]{3,2,1,0:T(8,128)(2,1)S(1)} %get-tuple-element.11.bt_ref, ...), custom_call_target="tpu_custom_call" | custom-call | tf_op jit(solution)/shard_map/finish/pallas_call | solution.py:673
